TPU v7x, 256 devices: a whole 4x4x8 slice. The times are simulated.
256 devices in a mesh: seq: 32 (over y, z_hi, x), grp: 8 (over z_lo, core).
Axes of the slice: x: 4, y: 4, z: 8 (z_hi: 2, z_lo: 4; z = z_hi * 4 + z_lo), core: 2. Of those that a mesh axis runs over, the one named last changes fastest.
Arguments:
- inputs: bfloat16 [4096, 8192], P('seq', 'grp'), may hold values from -10 to 10
- query_states: bfloat16 [4096, 8192], P('seq', 'grp'), may hold values from -12 to 12
- key_states: bfloat16 [4096, 1024], P('seq', 'grp'), may hold values from -6 to 6
- value_states: bfloat16 [4096, 1024], P('seq', 'grp'), may hold values from -6 to 6
- doc_ids: int32 [4096], replicated, may hold values from 0 to 7, never falling along the last dimension, each value on 1 to 3072 neighbouring positions
- modality: int32 [4096], P('seq'), may hold values from 0 to 1, as said below
- expert_ids: int32 [4096, 4], P('seq'), may hold values from -1 to 31, as said below
- norm_gain: float32 [8192], P('grp'), may hold values from 0.1 to 1.9
- router_w: bfloat16 [8192, 64], P('grp'), may hold values from -0.0625 to 0.0625
- w_in: bfloat16 [2, 32, 8192, 1408], P(None, 'seq', 'grp'), may hold values from -1 to 1
- w_out: bfloat16 [2, 32, 1408, 8192], P(None, 'seq', None, 'grp'), may hold values from -2 to 2
- grad_out: bfloat16 [4096, 8192], P('seq', 'grp'), may hold values from -12 to 12
Outputs:
- layer_out: bfloat16 [4096, 8192], P('seq', 'grp')
- state_grad: bfloat16 [4096, 8192], P('seq', 'grp')
Inputs may be any that keep to these rules, and one draw needn't show every extreme that they name: Modality is constant over aligned runs of 16 tokens; every block of 128 tokens held by one index of seq has a run of each modality. `expert_ids`: -1 marks an empty choice; the other entries of a token are distinct experts of its modality. At most 16 choices of the 128 tokens of one index of seq name one expert of one modality, and in every draw one text expert and one image expert are named by exactly 16 choices of every such block.
All inputs are finite; a program needn't handle non-finite values.
Results may differ from a plain program's by a relative error of at most 0.008.
Values may be sent and summed in bfloat16 or wider, within the bound.
A program may use at most 128 MiB of HBM per device.

v0:
```python
import jax
import jax.numpy as jnp
from jax import lax
from jax.sharding import PartitionSpec as P

D = 8192
HEADS = 64
KV_HEADS = 8
HEAD_DIM = 128
FF = 1408
TOP = 4
CAP = 16


eps_norm = 1e-05
gate_offset = 0.5


def gelu_back(pre_act, grad_in):
    return jax.vjp(lambda inner: jax.nn.gelu(inner, approximate=True), pre_act)[1](grad_in)[0]


def row_total(partial_value):
    return lax.psum(partial_value, "grp")


def dispatch(buffers):
    return lax.all_to_all(buffers, "seq", split_axis=1, concat_axis=1, tiled=True)


def collect(buffers):
    return lax.all_to_all(buffers, "seq", split_axis=1, concat_axis=1, tiled=True)


def hidden_step(partial_value, finish):
    summed = lax.psum(partial_value.astype(jnp.bfloat16), "grp").astype(jnp.float32)
    return finish(summed)


def attend(query_states, key_states, value_states, doc_ids):
    length = query_states.shape[0]
    kv_local = key_states.shape[1] // HEAD_DIM
    group_size = HEADS // KV_HEADS
    query_heads = query_states.reshape(length, kv_local, group_size, HEAD_DIM)
    first_query = lax.axis_index("seq") * length
    query_pos = first_query + jnp.arange(length, dtype=jnp.int32)
    query_doc = lax.dynamic_slice_in_dim(doc_ids, first_query, length)
    score_scale = HEAD_DIM ** (-0.5)
    key_piece = lax.all_gather(key_states, "seq", axis=0, tiled=True)
    value_piece = lax.all_gather(value_states, "seq", axis=0, tiled=True)
    piece_rows = key_piece.shape[0]
    best_score = jnp.full((length, kv_local, group_size), -1e30, jnp.float32)
    key_heads = key_piece.reshape(piece_rows, kv_local, HEAD_DIM)
    value_heads = value_piece.reshape(piece_rows, kv_local, HEAD_DIM).astype(jnp.float32)
    scores = (
        jnp.einsum("qhgd,khd->qhgk", query_heads, key_heads, preferred_element_type=jnp.float32)
        * score_scale
    )
    key_pos = jnp.arange(piece_rows, dtype=jnp.int32)
    allowed = (key_pos[None, :] <= query_pos[:, None]) & (doc_ids[None, :] == query_doc[:, None])
    allowed = allowed[:, None, None, :]
    scores = jnp.where(allowed, scores, -1e30)
    new_best = jnp.maximum(best_score, jnp.max(scores, axis=3))
    weights = jnp.where(allowed, jnp.exp(scores - new_best[..., None]), 0.0)
    totals = jnp.sum(weights, axis=3)
    summed = jnp.einsum("qhgk,khd->qhgd", weights, value_heads, precision=lax.Precision.HIGHEST)
    best_score, totals, summed = (new_best, totals, summed)
    return (
        (summed / totals[..., None])
        .reshape(length, kv_local * group_size * HEAD_DIM)
        .astype(jnp.bfloat16)
    )


def body(
    inputs,
    query_states,
    key_states,
    value_states,
    doc_ids,
    modality,
    expert_ids,
    norm_gain,
    router_w,
    w_in,
    w_out,
    grad_out,
):
    length, width_local = inputs.shape
    experts = lax.axis_size("seq")
    slot_total = 2 * experts * CAP
    attended = attend(query_states, key_states, value_states, doc_ids)
    resid_state = (inputs.astype(jnp.float32) + attended.astype(jnp.float32)).astype(jnp.bfloat16)
    state_wide = resid_state.astype(jnp.float32)
    squares = row_total(jnp.sum(state_wide * state_wide, axis=1))
    inv_rms = lax.rsqrt(squares / D + eps_norm)[:, None]
    scaled = state_wide * norm_gain[None, :]
    normed = (scaled * inv_rms).astype(jnp.bfloat16)
    logits = row_total(jnp.dot(normed, router_w, preferred_element_type=jnp.float32))
    kept_mask = expert_ids >= 0
    kept_wide = kept_mask.astype(jnp.float32)
    column = modality[:, None] * experts + jnp.where(kept_mask, expert_ids, 0)
    one_hot = (
        column[:, :, None] == jnp.arange(2 * experts, dtype=jnp.int32)[None, None, :]
    ) & kept_mask[:, :, None]
    chosen = jnp.sum(jnp.where(one_hot, logits[:, None, :], 0.0), axis=2)
    lifted = jax.nn.sigmoid(chosen)
    denominator = gate_offset + jnp.sum(kept_wide * lifted, axis=1, keepdims=True)
    gates = kept_wide * lifted / denominator
    entries = length * TOP
    flat_hot = one_hot.reshape(entries, 2 * experts).astype(jnp.bfloat16)
    entry_range = jnp.arange(entries, dtype=jnp.int32)
    earlier = (entry_range[:, None] > entry_range[None, :]).astype(jnp.bfloat16)
    before = jnp.dot(earlier, flat_hot, preferred_element_type=jnp.float32)
    slot_rank = jnp.sum(before * flat_hot.astype(jnp.float32), axis=1).astype(jnp.int32)
    slot_index = column.reshape(entries) * CAP + slot_rank
    table = (
        slot_index[:, None] == jnp.arange(slot_total, dtype=jnp.int32)[None, :]
    ) & kept_mask.reshape(entries)[:, None]
    table = table.astype(jnp.bfloat16).reshape(length, TOP, slot_total)
    token_table = jnp.sum(table, axis=1)
    w_in_local = w_in[:, 0]
    w_out_local = w_out[:, 0]
    sent_rows = jnp.einsum("ts,td->sd", token_table, normed, preferred_element_type=jnp.float32)
    sent_rows = sent_rows.astype(jnp.bfloat16).reshape(2, experts, CAP, width_local)
    got_rows = dispatch(sent_rows)
    partial_value = jnp.einsum(
        "ohn,ons->ohs",
        got_rows.reshape(2, experts * CAP, width_local),
        w_in_local,
        preferred_element_type=jnp.float32,
    ).reshape(2, experts, CAP, FF)

    def forward_finish(pre_act):
        return (jax.nn.gelu(pre_act, approximate=True).astype(jnp.bfloat16), pre_act)

    active, saved_pre = hidden_step(partial_value, forward_finish)
    expert_out = jnp.einsum(
        "nuv,nvg->nug",
        active.reshape(2, experts * CAP, FF),
        w_out_local,
        preferred_element_type=jnp.float32,
    ).astype(jnp.bfloat16)
    returned = collect(expert_out.reshape(2, experts, CAP, width_local)).reshape(
        slot_total, width_local
    )
    entry_out = jnp.einsum("tks,sd->tkd", table, returned, preferred_element_type=jnp.float32)
    mixture = jnp.sum(gates[:, :, None] * entry_out, axis=1)
    layer_out = (state_wide + mixture).astype(jnp.bfloat16)
    grad_wide = grad_out.astype(jnp.float32)
    gate_grad = row_total(jnp.sum(grad_wide[:, None, :] * entry_out, axis=2))
    gate_dot = jnp.sum(gates * gate_grad, axis=1, keepdims=True)
    logit_grad = kept_wide * (gate_grad - gate_dot) / denominator * lifted * (1.0 - lifted)
    logit_full = jnp.sum(jnp.where(one_hot, logit_grad[:, :, None], 0.0), axis=1)
    router_grad = jnp.dot(
        logit_full, router_w.astype(jnp.float32).T, precision=lax.Precision.HIGHEST
    )
    slot_gate = jnp.einsum(
        "tks,tk->s", table.astype(jnp.float32), gates, precision=lax.Precision.HIGHEST
    )
    grad_rows = (
        jnp.einsum("ts,td->sd", token_table, grad_out, preferred_element_type=jnp.float32)
        * slot_gate[:, None]
    )
    grad_rows = grad_rows.astype(jnp.bfloat16).reshape(2, experts, CAP, width_local)
    got_grads = dispatch(grad_rows)
    partial_back = jnp.einsum(
        "ukx,utx->ukt",
        got_grads.reshape(2, experts * CAP, width_local),
        w_out_local,
        preferred_element_type=jnp.float32,
    ).reshape(2, experts, CAP, FF)

    def backward_finish(act_grad):
        return (gelu_back(saved_pre, act_grad).astype(jnp.bfloat16), saved_pre)

    pre_grad = hidden_step(partial_back, backward_finish)[0]
    entry_grad = jnp.einsum(
        "upj,uoj->upo",
        pre_grad.reshape(2, experts * CAP, FF),
        w_in_local,
        preferred_element_type=jnp.float32,
    ).astype(jnp.bfloat16)
    grad_back = collect(entry_grad.reshape(2, experts, CAP, width_local)).reshape(
        slot_total, width_local
    )
    normed_grad = router_grad + jnp.einsum(
        "ts,sd->td", token_table, grad_back, preferred_element_type=jnp.float32
    )
    norm_dot = row_total(jnp.sum(normed_grad * scaled, axis=1))[:, None]
    state_grad = (
        grad_wide
        + inv_rms * norm_gain[None, :] * normed_grad
        - inv_rms**3 / D * state_wide * norm_dot
    )
    return (layer_out, state_grad.astype(jnp.bfloat16))


def solution(mesh):
    in_specs = (
        P("seq", "grp"),
        P("seq", "grp"),
        P("seq", "grp"),
        P("seq", "grp"),
        P(),
        P("seq"),
        P("seq", None),
        P("grp"),
        P("grp", None),
        P(None, "seq", "grp", None),
        P(None, "seq", None, "grp"),
        P("seq", "grp"),
    )
    out_specs = (P("seq", "grp"), P("seq", "grp"))
    return jax.shard_map(body, mesh=mesh, in_specs=in_specs, out_specs=out_specs, check_vma=False)
```

profile of v0, /device:TPU:1, one launch (start us, length us, event | category | flops | bytes accessed | tf_op | source)
XLA Modules:
  0.0 651.5 jit_solution(6634678139856003361)
XLA Ops:
  7.2 0.0 copy-start
  7.2 0.0 all-gather.3.cloned.1.call-start
  7.2 0.7 all-gather.3.cloned.1.call-update
  7.9 0.0 all-gather.5.cloned.1.call-start
  8.0 1.5 copy.76
  9.4 0.0 all-gather.5.cloned.1.call-update
  9.5 0.7 broadcast_multiply_fusion
  10.1 0.7 select_add_fusion
  10.8 0.1 copy.80
  11.0 0.1 and.55
  11.1 0.1 copy.79
  11.2 0.1 eq.79
  11.3 0.3 fusion.52
  11.6 0.1 convert_element_type.109
  11.7 0.1 copy.81
  11.8 0.5 fusion.53
  12.3 0.8 dynamic_slice.3
  13.0 2.5 fusion.34
  15.5 79.9 %all-gather.3.cloned.1.call-done = bf16[4096,128]{1,0:T(8,128)(2,1)} async-done(((bf16[128,128]{1,0:T(8,128)(2,1)}), bf16[4096,128]{1,0:T(8,128)(2,1)}) %all-gather.3.cloned.1.call-update) | async-done | bytes 1048592 | tf_op jit(solution)/shard_map/all_gather | solution.py:49
  95.4 3.8 fusion.2
  99.2 5.7 copy-done.2
  104.9 4.0 fusion.3
  109.0 0.0 copy-start.7
  109.0 0.0 copy-start.4
  109.0 68.1 %all-gather.5.cloned.1.call-done = bf16[4096,128]{0,1:T(8,128)(2,1)} async-done(((bf16[128,128]{0,1:T(8,128)(2,1)}), bf16[4096,128]{0,1:T(8,128)(2,1)}) %all-gather.5.cloned.1.call-update) | async-done | bytes 1048592 | tf_op jit(solution)/shard_map/all_gather | solution.py:50
  177.2 12.9 %fusion.71 = f32[1,128,128,8]{2,1,3,0:T(8,128)S(1)} fusion(bf16[4096,128]{0,1:T(8,128)(2,1)} %all-gather.5.cloned.1.call-done, f32[4096,128,8]{1,0,2:T(8,128)} %copy-done.2, f32[128,8]{0,1:T(8,128)S(1)} %broadcast_maximum_fusion, pred[128,4096]{0,1:T(8,128)(4,1)S(1)} %fusion.34, f32[128,8]{0,1:T(8,128)S(1)} %fusion.3), kind=kOutput, calls=%fused_computation.69 | convolution fusion | flops 6459621376 | bytes 18882560 | tf_op jit(solution)/shard_map/qhgk,khd->qhgd/dot_general | solution.py:66
  190.1 0.2 copy.78
  190.3 0.2 fusion.80
  190.5 15.0 %psum.42 = f32[128]{0:T(128)S(1)} all-reduce(f32[128]{0:T(128)S(1)} %get-tuple-element.6), channel_id=1, replica_groups=mesh['seq'=32,'grp'=8] {'grp'}, use_global_device_ids=true, to_apply=%region_3.4 | all-reduce | flops 128 | bytes 1024 | tf_op jit(solution)/shard_map/psum | solution.py:24
  205.5 0.3 fusion.92
  205.8 22.5 %psum.43 = f32[128,64]{0,1:T(8,128)S(1)} all-reduce(f32[128,64]{0,1:T(8,128)S(1)} %fusion.92), channel_id=1, replica_groups=mesh['seq'=32,'grp'=8] {'grp'}, use_global_device_ids=true, to_apply=%region_4.5 | all-reduce | flops 8192 | bytes 65536 | tf_op jit(solution)/shard_map/psum | solution.py:24
  228.4 0.9 fusion.40
  229.3 0.8 multiply_convert_fusion
  230.0 1.5 copy.86
  231.5 6.3 all-to-all-start.2
  237.8 0.8 convolution_convert_fusion
  238.6 1.5 copy.82
  240.1 47.7 %all-to-all-done.2 = bf16[2,32,16,1024]{3,2,0,1:T(8,128)(2,1)S(1)} async-done(((bf16[2,32,16,1024]{3,2,0,1:T(8,128)(2,1)}), bf16[2,32,16,1024]{3,2,0,1:T(8,128)(2,1)S(1)}, u32[]{:S(2)}, u32[]{:S(2)}) %all-to-all-start.2) | async-done | bytes 2097184 | tf_op jit(solution)/shard_map/all_to_all | solution.py:28
  287.8 8.5 %all-to-all-start = ((bf16[2,32,16,1024]{3,2,0,1:T(8,128)(2,1)}), bf16[2,32,16,1024]{3,2,0,1:T(8,128)(2,1)}, u32[]{:S(2)}, u32[]{:S(2)}) async-start(bf16[2,32,16,1024]{3,2,0,1:T(8,128)(2,1)} %copy.82), calls=%async_computation | async-start | bytes 4194304 | tf_op jit(solution)/shard_map/all_to_all | solution.py:28
  296.4 0.0 all-reduce.3.cloned.1.call-start
  296.4 0.3 copy.87
  296.7 7.5 %fusion.31 = bf16[2,512,1408]{2,1,0:T(8,128)(2,1)} fusion(bf16[2,512,1024]{2,1,0:T(8,128)(2,1)S(1)} %bitcast.131, bf16[2,1,1408,1024]{3,2,1,0:T(8,128)(2,1)} %param.22), kind=kOutput, calls=%fused_computation.38 | convolution fusion | flops 2954231808 | bytes 10747904 | tf_op jit(solution)/shard_map/ukx,utx->ukt/dot_general | solution.py:167
  304.2 40.7 %all-to-all-done = bf16[2,32,16,1024]{3,2,0,1:T(8,128)(2,1)} async-done(((bf16[2,32,16,1024]{3,2,0,1:T(8,128)(2,1)}), bf16[2,32,16,1024]{3,2,0,1:T(8,128)(2,1)}, u32[]{:S(2)}, u32[]{:S(2)}) %all-to-all-start) | async-done | bytes 2097184 | tf_op jit(solution)/shard_map/all_to_all | solution.py:28
  344.8 1.8 copy.83
  346.7 7.4 %fusion.28 = bf16[2,512,1408]{2,1,0:T(8,128)(2,1)} fusion(bf16[2,512,1024]{2,1,0:T(8,128)(2,1)S(1)} %bitcast.132, bf16[2,1,1024,1408]{3,2,1,0:T(8,128)(2,1)} %param.21), kind=kOutput, calls=%fused_computation.37 | convolution fusion | flops 2954231808 | bytes 10747904 | tf_op jit(solution)/shard_map/ohn,ons->ohs/dot_general | solution.py:127
  354.1 0.0 all-reduce.3.cloned.1.call-update
  354.1 135.9 %all-reduce.3.cloned.1.call-done = (bf16[2,32,16,1408]{3,2,1,0:T(8,128)(2,1)}, bf16[2,32,16,1408]{3,2,1,0:T(8,128)(2,1)}) async-done(((bf16[2,32,16,1408]{3,2,1,0:T(8,128)(2,1)}, bf16[2,32,16,1408]{3,2,1,0:T(8,128)(2,1)}), (bf16[2,32,16,1408]{3,2,1,0:T(8,128)(2,1)}, bf16[2,32,16,1408]{3,2,1,0:T(8,128)(2,1)})) %all-reduce.3.cloned.1.call-update) | async-done | bytes 5767184 | tf_op jit(solution)/shard_map/psum | solution.py:36
  490.0 7.6 %fusion.12 = (bf16[2,32,16,1408]{3,2,1,0:T(8,128)(2,1)}, bf16[2,32,16,1408]{3,2,1,0:T(8,128)(2,1)S(1)}) fusion(bf16[2,32,16,1408]{3,2,1,0:T(8,128)(2,1)} %get-tuple-element.5, bf16[2,32,16,1408]{3,2,1,0:T(8,128)(2,1)} %get-tuple-element.4), kind=kLoop, calls=%fused_computation.20 | loop fusion | flops 34603008 | bytes 11534336 | tf_op jit(solution)/shard_map/convert_element_type | solution.py:175
  497.6 3.7 fusion.46
  501.4 1.6 copy.84
  503.0 11.7 %all-to-all-start.1 = ((bf16[2,32,16,1024]{3,2,0,1:T(8,128)(2,1)}), bf16[2,32,16,1024]{3,2,0,1:T(8,128)(2,1)S(1)}, u32[]{:S(2)}, u32[]{:S(2)}) async-start(bf16[2,32,16,1024]{3,2,0,1:T(8,128)(2,1)} %copy.84), calls=%async_computation.1 | async-start | bytes 4194304 | tf_op jit(solution)/shard_map/all_to_all | solution.py:32
  514.6 7.0 %fusion.43 = bf16[2,512,1024]{2,1,0:T(8,128)(2,1)S(1)} fusion(bf16[2,512,1408]{2,1,0:T(8,128)(2,1)} %bitcast.128, bf16[2,1,1024,1408]{3,2,1,0:T(8,128)(2,1)} %param.21), kind=kOutput, calls=%fused_computation.51 | convolution fusion | flops 2953838592 | bytes 10747904 | tf_op jit(solution)/shard_map/upj,uoj->upo/dot_general | solution.py:178
  521.6 1.7 copy.88
  523.3 39.5 %all-to-all-done.1 = bf16[2,32,16,1024]{3,2,0,1:T(8,128)(2,1)S(1)} async-done(((bf16[2,32,16,1024]{3,2,0,1:T(8,128)(2,1)}), bf16[2,32,16,1024]{3,2,0,1:T(8,128)(2,1)S(1)}, u32[]{:S(2)}, u32[]{:S(2)}) %all-to-all-start.1) | async-done | bytes 2097184 | tf_op jit(solution)/shard_map/all_to_all | solution.py:32
  562.8 1.3 copy-done.3
  564.1 7.0 %all-to-all-start.3 = ((bf16[2,32,16,1024]{3,2,0,1:T(8,128)(2,1)}), bf16[2,32,16,1024]{3,2,0,1:T(8,128)(2,1)S(1)}, u32[]{:S(2)}, u32[]{:S(2)}) async-start(bf16[2,32,16,1024]{3,2,0,1:T(8,128)(2,1)} %copy.88), calls=%async_computation.3 | async-start | bytes 4194304 | tf_op jit(solution)/shard_map/all_to_all | solution.py:32
  571.1 1.8 copy.85
  572.9 2.2 multiply_reduce_fusion
  575.1 50.6 %psum.45 = f32[128,4]{0,1:T(4,128)S(1)} all-reduce(f32[128,4]{0,1:T(4,128)S(1)} %get-tuple-element.2), channel_id=1, replica_groups=mesh['seq'=32,'grp'=8] {'grp'}, use_global_device_ids=true, to_apply=%region_12.13 | all-reduce | flops 512 | bytes 4096 | tf_op jit(solution)/shard_map/psum | solution.py:24
  625.8 0.2 copy.89
  626.0 0.5 fusion.102
  626.4 0.6 fusion.79
  627.0 15.9 %psum.47 = f32[128]{0:T(128)S(1)} all-reduce(f32[128]{0:T(128)S(1)} %get-tuple-element.18), channel_id=1, replica_groups=mesh['seq'=32,'grp'=8] {'grp'}, use_global_device_ids=true, to_apply=%region_17.18 | all-reduce | flops 128 | bytes 1024 | tf_op jit(solution)/shard_map/psum | solution.py:24
  642.9 2.1 fusion.84
  (30 shorter events, 0.3 us)
Async XLA Ops:
  7.2 88.2 %copy-start = (bf16[128,1024]{1,0:T(8,128)(2,1)S(1)}, bf16[128,1024]{1,0:T(8,128)(2,1)}, u32[]{:S(2)}) copy-start(bf16[128,1024]{1,0:T(8,128)(2,1)} %param.13) | copy-start | bytes 786436
  7.2 88.2 %all-gather.3.cloned.1.call-start = ((), (), s32[]{:S(2)}) async-start(), calls=%async_computation.4 | async-start | bytes 1081344 | tf_op jit(solution)/shard_map/all_gather | solution.py:49
  7.9 169.2 %all-gather.5.cloned.1.call-start = ((), (), s32[]{:S(2)}) async-start(), calls=%async_computation.5 | async-start | bytes 1081344 | tf_op jit(solution)/shard_map/all_gather | solution.py:50
  99.2 5.7 copy-start.2
  109.0 81.3 %copy-start.5 = (bf16[128,1024]{1,0:T(8,128)(2,1)S(1)}, bf16[128,1024]{1,0:T(8,128)(2,1)}, u32[]{:S(2)}) copy-start(bf16[128,1024]{1,0:T(8,128)(2,1)} %param.12) | copy-start | bytes 786436
  109.0 96.5 %copy-start.6 = (bf16[1024,64]{0,1:T(8,128)(2,1)S(1)}, bf16[1024,64]{0,1:T(8,128)(2,1)}, u32[]{:S(2)}) copy-start(bf16[1024,64]{0,1:T(8,128)(2,1)} %param.20) | copy-start | bytes 393220
  109.0 96.5 %copy-start.7 = (f32[1024]{0:T(1024)S(1)}, f32[1024]{0:T(1024)}, u32[]{:S(2)}) copy-start(f32[1024]{0:T(1024)} %param.19) | copy-start | bytes 12292
  109.0 120.3 %copy-start.4 = (bf16[128,1024]{1,0:T(8,128)(2,1)S(1)}, bf16[128,1024]{1,0:T(8,128)(2,1)}, u32[]{:S(2)}) copy-start(bf16[128,1024]{1,0:T(8,128)(2,1)} %param.23) | copy-start | bytes 786436
  231.5 56.3 %all-to-all-start.2 = ((bf16[2,32,16,1024]{3,2,0,1:T(8,128)(2,1)}), bf16[2,32,16,1024]{3,2,0,1:T(8,128)(2,1)S(1)}, u32[]{:S(2)}, u32[]{:S(2)}) async-start(bf16[2,32,16,1024]{3,2,0,1:T(8,128)(2,1)} %copy.86), calls=%async_computation.2 | async-start | bytes 4194304 | tf_op jit(solution)/shard_map/all_to_all | solution.py:28
  287.8 57.0 %all-to-all-start = ((bf16[2,32,16,1024]{3,2,0,1:T(8,128)(2,1)}), bf16[2,32,16,1024]{3,2,0,1:T(8,128)(2,1)}, u32[]{:S(2)}, u32[]{:S(2)}) async-start(bf16[2,32,16,1024]{3,2,0,1:T(8,128)(2,1)} %copy.82), calls=%async_computation | async-start | bytes 4194304 | tf_op jit(solution)/shard_map/all_to_all | solution.py:28
  296.4 193.6 %all-reduce.3.cloned.1.call-start = ((), (), s32[]{:S(2)}) async-start(), calls=%async_computation.6 | async-start | bytes 11534336 | tf_op jit(solution)/shard_map/psum | solution.py:36
  354.1 143.5 %slice-start = ((s8[5767168]{0:T(1024)(128)(4,1)}), s8[1572864]{0:T(1024)(128)(4,1)S(1)}, s32[]{:S(2)}) async-start(s8[5767168]{0:T(1024)(128)(4,1)} %bitcast.138), calls=%async_computation.7 | async-start | bytes 3145728
  490.0 7.6 %slice-start.1 = ((s8[5767168]{0:T(1024)(128)(4,1)}), s8[4194304]{0:T(1024)(128)(4,1)S(1)}, s32[]{:S(2)}) async-start(s8[5767168]{0:T(1024)(128)(4,1)} %bitcast.138), calls=%async_computation.8 | async-start | bytes 8388608
  503.0 59.8 %all-to-all-start.1 = ((bf16[2,32,16,1024]{3,2,0,1:T(8,128)(2,1)}), bf16[2,32,16,1024]{3,2,0,1:T(8,128)(2,1)S(1)}, u32[]{:S(2)}, u32[]{:S(2)}) async-start(bf16[2,32,16,1024]{3,2,0,1:T(8,128)(2,1)} %copy.84), calls=%async_computation.1 | async-start | bytes 4194304 | tf_op jit(solution)/shard_map/all_to_all | solution.py:32
  562.8 1.3 copy-start.3
  564.1 61.7 %all-to-all-start.3 = ((bf16[2,32,16,1024]{3,2,0,1:T(8,128)(2,1)}), bf16[2,32,16,1024]{3,2,0,1:T(8,128)(2,1)S(1)}, u32[]{:S(2)}, u32[]{:S(2)}) async-start(bf16[2,32,16,1024]{3,2,0,1:T(8,128)(2,1)} %copy.88), calls=%async_computation.3 | async-start | bytes 4194304 | tf_op jit(solution)/shard_map/all_to_all | solution.py:32
  625.8 19.2 %copy-start.1 = (bf16[128,1024]{1,0:T(8,128)(2,1)S(1)}, bf16[128,1024]{1,0:T(8,128)(2,1)}, u32[]{:S(2)}) copy-start(bf16[128,1024]{1,0:T(8,128)(2,1)} %param.13) | copy-start | bytes 786436
Sparse Core Ops, SparseCore 0:
  11.4 83.9 all-gather.2
  99.2 77.9 all-gather.4
  354.2 135.7 all-reduce.2
where the time goes:
time: 652 us
  waiting for transfers between devices  413 us (63%)
  blocking collectives  104 us (16%)
  matrix products  48.5 us (7%)
  starting transfers between devices  33.5 us (5%)
  local copies, waits for them, and re-layouts  20.5 us (3%)
  other arithmetic  18.4 us (3%)
  between operations  14 us (2%)
    psum x1, waiting for transfers between devices, hidden_step(): lax.psum(partial_value.astype(jnp.bfloat16), 'grp').astype(jnp.float32)  136 us
    psum x4, blocking collectives, row_total(): return lax.psum(partial_value, 'grp')  104 us
    all_to_all x2, waiting for transfers between devices, dispatch(): lax.all_to_all(buffers, 'seq', split_axis=1, concat_axis=1, tiled=True)  88.4 us
    all_gather x1, waiting for transfers between devices, attend(): key_piece = lax.all_gather(key_states, 'seq', axis=0, tiled=True)  79.9 us
    all_gather x1, waiting for transfers between devices, attend(): value_piece = lax.all_gather(value_states, 'seq', axis=0, tiled=True)  68.1 us
    all_to_all x2, waiting for transfers between devices, collect(): lax.all_to_all(buffers, 'seq', split_axis=1, concat_axis=1, tiled=True)  39.5 us
    all_to_all x2, starting transfers between devices, collect(): lax.all_to_all(buffers, 'seq', split_axis=1, concat_axis=1, tiled=True)  18.6 us
    all_to_all x2, starting transfers between devices, dispatch(): lax.all_to_all(buffers, 'seq', split_axis=1, concat_axis=1, tiled=True)  14.8 us
  transfers between devices with their start and end apart: 7, of which 6 were waited for; matrix products, arithmetic and copies ran while one was open for 6% of the time, Pallas kernels for 0%

commit v1 on v0

v1 whole, which is shorter than its diff:
```python
import functools

import jax
import jax.numpy as jnp
from jax import lax
from jax.experimental import pallas as pl
from jax.experimental.pallas import tpu as pltpu
from jax.sharding import PartitionSpec as P

D = 8192
HEADS = 64
KV_HEADS = 8
HEAD_DIM = 128
FF = 1408
TOP = 4
CAP = 16
LEN = 128
WIDTH = 1024

eps_norm = 1e-05
gate_offset = 0.5

MESH = pl.DeviceIdType.MESH
VMEM = pl.BlockSpec(memory_space=pltpu.VMEM)
ANY = pl.BlockSpec(memory_space=pl.ANY)
LIMIT = 56 * 1024 * 1024


def params(collective_id=None):
    if collective_id is None:
        return pltpu.CompilerParams(vmem_limit_bytes=LIMIT)
    return pltpu.CompilerParams(
        collective_id=collective_id, has_side_effects=True, vmem_limit_bytes=LIMIT
    )


class Links:
    def __init__(self, send, recv):
        self.send, self.recv = send, recv
        self.used = 0
        self.started = []

    def ids(self, count):
        first = self.used
        self.used += count
        return [first + i for i in range(count)]

    def copy(self, src, dst, index, axis, peer):
        return pltpu.make_async_remote_copy(
            src_ref=src,
            dst_ref=dst,
            send_sem=self.send.at[index],
            recv_sem=self.recv.at[index],
            device_id={axis: peer},
            device_id_type=MESH,
        )

    def start(self, src, dst, index, axis, peer):
        copy = self.copy(src, dst, index, axis, peer)
        copy.start()
        self.started.append(copy)
        return copy

    def local(self, src, dst, index):
        copy = pltpu.make_async_copy(src, dst, self.send.at[index])
        copy.start()
        return copy

    def finish(self):
        for copy in self.started:
            copy.wait_send()


def greet(axis, peers):
    barrier = pltpu.get_barrier_semaphore()
    for peer in peers:
        pl.semaphore_signal(barrier, inc=1, device_id={axis: peer}, device_id_type=MESH)
    pl.semaphore_wait(barrier, len(peers))


class Place:
    def __init__(self):
        me = lax.axis_index("seq")
        self.y, self.rest = me // 8, me % 8
        self.z, self.x = self.rest // 4, self.rest % 4
        self.zp = self.at(z=1 - self.z)
        self.xr, self.xl = self.at(x=(self.x + 1) % 4), self.at(x=(self.x + 3) % 4)
        self.yr, self.yl = self.at(y=(self.y + 1) % 4), self.at(y=(self.y + 3) % 4)
        self.y_next, self.y_prev, self.y_far = (self.y + 1) % 4, (self.y + 3) % 4, (self.y + 2) % 4

    def at(self, y=None, z=None, x=None):
        y = self.y if y is None else y
        z = self.z if z is None else z
        x = self.x if x is None else x
        return y * 8 + z * 4 + x

    def block(self, z, shift):
        return z * 4 + (self.x + shift) % 4


def slot_codes(rest):
    row = lax.broadcasted_iota(jnp.int32, (LEN, LEN), 0)
    owner = (row // 32) * 8 + rest
    return (((row // 16) % 2) * 32 + owner) * CAP + row % 16


def kv_kernel(kv_in, kv_out, send, recv):
    here = Place()
    links = Links(send, recv)
    me = here.at()
    greet("seq", [here.zp, here.xr, here.xl, here.yr, here.yl])
    own_id, z_id = links.ids(2)
    x1r, x1l, x2r, x2l = links.ids(2), links.ids(2), links.ids(2), links.ids(2)
    yr_id, yl_id, f_id = links.ids(8), links.ids(8), links.ids(8)
    own = links.local(kv_in, kv_out.at[me], own_id)
    half = LEN // 2

    def spot(z, shift, y=None):
        return kv_out.at[here.at(y=y, z=z, x=(here.x + shift) % 4)]

    def y_send(order, src, dst):
        r = links.start(src, dst, yr_id[order], "seq", here.yr)
        l = links.start(src, dst, yl_id[order], "seq", here.yl)
        return r, l

    zc = links.start(kv_in, spot(here.z, 0), z_id, "seq", here.zp)
    sent = {}
    zs = [here.z, 1 - here.z]
    first = [None, None]
    second = [None, None]
    first[0] = (
        links.start(kv_in, spot(zs[0], 0), x1r[0], "seq", here.xr),
        links.start(kv_in, spot(zs[0], 0), x1l[0], "seq", here.xl),
    )
    sent[0] = y_send(0, kv_in, spot(zs[0], 0))

    def forward_x(p):
        z = zs[p]
        first[p][0].wait_recv()
        left = spot(z, 3)
        a = links.start(left.at[pl.ds(0, half)], left.at[pl.ds(0, half)], x2r[p], "seq", here.xr)
        sent[p * 4 + 1] = y_send(p * 4 + 1, left, left)
        first[p][1].wait_recv()
        right = spot(z, 1)
        b = links.start(
            right.at[pl.ds(half, half)], right.at[pl.ds(half, half)], x2l[p], "seq", here.xl
        )
        sent[p * 4 + 2] = y_send(p * 4 + 2, right, right)
        second[p] = (a, b)

    def far_x(p):
        second[p][0].wait_recv()
        second[p][1].wait_recv()
        far = spot(zs[p], 2)
        sent[p * 4 + 3] = y_send(p * 4 + 3, far, far)

    shifts = [0, 3, 1, 2]
    forwarded = []

    def forward_y(order):
        z, shift = zs[order // 4], shifts[order % 4]
        if order % 2 == 0:
            sent[order][0].wait_recv()
            piece = spot(z, shift, here.y_prev)
            forwarded.append(links.start(piece, piece, f_id[order], "seq", here.yr))
        else:
            sent[order][1].wait_recv()
            piece = spot(z, shift, here.y_next)
            forwarded.append(links.start(piece, piece, f_id[order], "seq", here.yl))

    forward_x(0)
    zc.wait_recv()
    other = spot(zs[1], 0)
    first[1] = (
        links.start(other, other, x1r[1], "seq", here.xr),
        links.start(other, other, x1l[1], "seq", here.xl),
    )
    sent[4] = y_send(4, other, other)
    forward_y(0)
    far_x(0)
    forward_y(1)
    forward_x(1)
    forward_y(2)
    far_x(1)
    for order in range(3, 8):
        forward_y(order)
    for order in range(8):
        sent[order][1 if order % 2 == 0 else 0].wait_recv()
    for copy in forwarded:
        copy.wait_recv()
    own.wait()
    links.finish()


KV_SEMS = 2 + 8 + 24


def gather_kv(kv):
    return pl.pallas_call(
        kv_kernel,
        name="gather_kv",
        out_shape=jax.ShapeDtypeStruct((32, LEN, 2 * HEAD_DIM), jnp.bfloat16),
        in_specs=[VMEM],
        out_specs=ANY,
        scratch_shapes=[pltpu.SemaphoreType.DMA((KV_SEMS,)), pltpu.SemaphoreType.DMA((KV_SEMS,))],
        compiler_params=params(0),
    )(kv)


def dispatch_kernel(share, *refs):
    if share:
        rows, slots, got, tokens, table, out_buf, far_buf, send, recv = refs
    else:
        rows, table, got, tokens, out_buf, far_buf, send, recv = refs
    here = Place()
    links = Links(send, recv)
    peers = [here.zp, here.xr, here.xl, here.yr, here.yl]
    if share:
        peers += [here.at(x=(here.x + 2) % 4)] + [
            here.at(z=1 - here.z, x=(here.x + shift) % 4) for shift in (1, 2, 3)
        ]
    zs = [here.z, 1 - here.z]
    shifts = [0, 3, 1, 2]
    half = LEN // 2
    (z_id,) = links.ids(1)
    x1r, x1l, x2r, x2l = links.ids(2), links.ids(2), links.ids(2), links.ids(2)
    yr_id, yl_id, f1_id, f2_id, own_id = (
        links.ids(8),
        links.ids(8),
        links.ids(8),
        links.ids(8),
        links.ids(8),
    )
    t_id = links.ids(8)
    greet("seq", peers)

    def spot(p, shift):
        return tokens.at[here.block(zs[p], shift)]

    mine = spot(0, 0)
    zc = links.start(rows, mine, z_id, "seq", here.zp)
    first = [None, None]
    second = [None, None]
    first[0] = (
        links.start(rows, mine, x1r[0], "seq", here.xr),
        links.start(rows, mine, x1l[0], "seq", here.xl),
    )
    if share:
        told = []
        for order in range(1, 8):
            peer = here.at(z=zs[order // 4], x=(here.x + shifts[order % 4]) % 4)
            told.append(
                links.start(slots, table.at[here.rest], t_id[order], "seq", peer)
            )
        table[here.rest] = slots[...]
    tokens[here.rest] = rows[...]
    codes = slot_codes(here.rest)
    sent = {}
    locals_ = []

    def pick(order):
        p, shift = order // 4, shifts[order % 4]
        block = here.block(zs[p], shift)
        ids = table[block]
        hot = jnp.zeros((LEN, LEN), jnp.float32)
        for k in range(TOP):
            hot = hot + jnp.where(ids[k : k + 1, :] == codes, 1.0, 0.0)
        picked = jnp.dot(
            hot.astype(jnp.bfloat16), tokens[block], preferred_element_type=jnp.float32
        )
        out_buf[:, :, block] = picked.astype(jnp.bfloat16).reshape(4, 2, CAP, WIDTH)
        place = got.at[:, here.y, block]
        a = links.start(
            out_buf.at[here.y_next, :, block], place, yr_id[order], "seq", here.yr
        )
        b = links.start(
            out_buf.at[here.y_prev, :, block], place, yl_id[order], "seq", here.yl
        )
        c = links.start(
            out_buf.at[here.y_far, :, block],
            far_buf.at[order],
            f1_id[order],
            "seq",
            here.yr if order % 2 == 0 else here.yl,
        )
        locals_.append(links.local(out_buf.at[here.y, :, block], place, own_id[order]))
        sent[order] = [a, b, c]

    def forward_y(order):
        p, shift = order // 4, shifts[order % 4]
        block = here.block(zs[p], shift)
        sent[order][2].wait_recv()
        source, target = (
            (here.y_prev, here.yr) if order % 2 == 0 else (here.y_next, here.yl)
        )
        sent[order].append(
            links.start(
                far_buf.at[order], got.at[:, source, block], f2_id[order], "seq", target
            )
        )

    def forward_x(p):
        first[p][0].wait_recv()
        left = spot(p, 3)
        a = links.start(left.at[pl.ds(0, half)], left.at[pl.ds(0, half)], x2r[p], "seq", here.xr)
        first[p][1].wait_recv()
        right = spot(p, 1)
        b = links.start(
            right.at[pl.ds(half, half)], right.at[pl.ds(half, half)], x2l[p], "seq", here.xl
        )
        second[p] = (a, b)

    def far_x(p):
        second[p][0].wait_recv()
        second[p][1].wait_recv()

    if share:
        for copy in told:
            copy.wait_recv()
    pick(0)
    forward_x(0)
    pick(1)
    pick(2)
    zc.wait_recv()
    other = spot(1, 0)
    first[1] = (
        links.start(other, other, x1r[1], "seq", here.xr),
        links.start(other, other, x1l[1], "seq", here.xl),
    )
    forward_y(0)
    pick(4)
    far_x(0)
    pick(3)
    forward_y(1)
    forward_y(2)
    forward_x(1)
    pick(5)
    pick(6)
    forward_y(4)
    forward_y(3)
    far_x(1)
    pick(7)
    for order in (5, 6, 7):
        forward_y(order)
    for order in range(8):
        sent[order][0].wait_recv()
        sent[order][1].wait_recv()
        sent[order][3].wait_recv()
    for copy in locals_:
        copy.wait()
    links.finish()


DISPATCH_SEMS = 1 + 8 + 40 + 8


def dispatch_first(rows, slots):
    return pl.pallas_call(
        functools.partial(dispatch_kernel, True),
        name="dispatch_grads",
        out_shape=(
            jax.ShapeDtypeStruct((2, 4, 8, CAP, WIDTH), jnp.bfloat16),
            jax.ShapeDtypeStruct((8, LEN, WIDTH), jnp.bfloat16),
            jax.ShapeDtypeStruct((8, 8, LEN), jnp.int32),
        ),
        in_specs=[VMEM, VMEM],
        out_specs=(ANY, VMEM, VMEM),
        scratch_shapes=[
            pltpu.VMEM((4, 2, 8, CAP, WIDTH), jnp.bfloat16),
            pltpu.VMEM((8, 2, CAP, WIDTH), jnp.bfloat16),
            pltpu.SemaphoreType.DMA((DISPATCH_SEMS,)),
            pltpu.SemaphoreType.DMA((DISPATCH_SEMS,)),
        ],
        compiler_params=params(1),
    )(rows, slots)


def dispatch_next(rows, table):
    return pl.pallas_call(
        functools.partial(dispatch_kernel, False),
        name="dispatch_rows",
        out_shape=jax.ShapeDtypeStruct((2, 4, 8, CAP, WIDTH), jnp.bfloat16),
        in_specs=[VMEM, VMEM],
        out_specs=ANY,
        scratch_shapes=[
            pltpu.VMEM((8, LEN, WIDTH), jnp.bfloat16),
            pltpu.VMEM((4, 2, 8, CAP, WIDTH), jnp.bfloat16),
            pltpu.VMEM((8, 2, CAP, WIDTH), jnp.bfloat16),
            pltpu.SemaphoreType.DMA((DISPATCH_SEMS,)),
            pltpu.SemaphoreType.DMA((DISPATCH_SEMS,)),
        ],
        compiler_params=params(2),
    )(rows, table)


def collect_kernel(forward, *refs):
    if forward:
        (
            results, table, gates, tokens, total, gates_all, gate_sum,
            back, part, far_buf, x_half, x_full, z_buf, grad_part, grad_got, send, recv,
        ) = refs
    else:
        (
            results, table, gates_all, total,
            back, part, far_buf, x_half, x_full, z_buf, send, recv,
        ) = refs
    here = Place()
    links = Links(send, recv)
    peers = [here.zp, here.xr, here.xl, here.yr, here.yl]
    if forward:
        peers += [here.at(x=(here.x + 2) % 4)] + [
            here.at(z=1 - here.z, x=(here.x + shift) % 4) for shift in (1, 2, 3)
        ]
    zs = [1 - here.z, here.z]
    shifts = [2, 1, 3, 0]
    half = LEN // 2
    (z_id,) = links.ids(1)
    hr, hl, fr, fl = links.ids(2), links.ids(2), links.ids(2), links.ids(2)
    yr_id, yl_id, f1_id, f2_id, own_id = (
        links.ids(8),
        links.ids(8),
        links.ids(8),
        links.ids(8),
        links.ids(8),
    )
    t_id, g_id = links.ids(8), links.ids(8)
    greet("seq", peers)
    blocks = [here.block(zs[order // 4], shifts[order % 4]) for order in range(8)]
    sent = {}
    locals_ = []
    for order in range(8):
        block = blocks[order]
        place = back.at[here.y, :, block]
        a = links.start(results.at[:, here.y_next, block], place, yr_id[order], "seq", here.yr)
        b = links.start(results.at[:, here.y_prev, block], place, yl_id[order], "seq", here.yl)
        c = links.start(
            results.at[:, here.y_far, block],
            far_buf.at[order],
            f1_id[order],
            "seq",
            here.yr if order % 2 == 0 else here.yl,
        )
        locals_.append(links.local(results.at[:, here.y, block], place, own_id[order]))
        sent[order] = [a, b, c]
    told = []
    if forward:
        for order in range(7):
            peer = here.at(z=zs[order // 4], x=(here.x + shifts[order % 4]) % 4)
            told.append(links.start(gates, gates_all.at[here.rest], t_id[order], "seq", peer))
        gates_all[here.rest] = gates[...]
        for copy in told:
            copy.wait_recv()
    codes = slot_codes(here.rest)

    def forward_y(order):
        sent[order][2].wait_recv()
        source, target = (
            (here.y_prev, here.yr) if order % 2 == 0 else (here.y_next, here.yl)
        )
        sent[order].append(
            links.start(
                far_buf.at[order], back.at[source, :, blocks[order]], f2_id[order], "seq", target
            )
        )

    grads_sent = []

    def combine(order):
        block = blocks[order]
        locals_[order].wait()
        for which in (0, 1, 3):
            sent[order][which].wait_recv()
        rows = back[:, :, block].reshape(LEN, WIDTH)
        ids = table[block]
        weight = gates_all[block]
        mix = jnp.zeros((LEN, LEN), jnp.float32)
        for k in range(TOP):
            mix = mix + jnp.where(ids[k : k + 1, :] == codes, weight[k : k + 1, :], 0.0)
        summed = lax.dot_general(
            mix.astype(jnp.bfloat16),
            rows,
            (((0,), (0,)), ((), ())),
            preferred_element_type=jnp.float32,
        )
        if forward:
            dots = lax.dot_general(
                rows, tokens[block], (((1,), (1,)), ((), ())), preferred_element_type=jnp.float32
            )
            for k in range(TOP):
                grad_part[order, k : k + 1, :] = jnp.sum(
                    jnp.where(ids[k : k + 1, :] == codes, dots, 0.0), axis=0, keepdims=True
                )
            grad_part[order, TOP:, :] = jnp.zeros((8 - TOP, LEN), jnp.float32)
            if order < 7:
                peer = here.at(z=zs[order // 4], x=(here.x + shifts[order % 4]) % 4)
                grads_sent.append(
                    links.start(
                        grad_part.at[order], grad_got.at[order], g_id[order], "seq", peer
                    )
                )
        return summed

    halves = [None, None]
    fulls = [[None, None], [None, None]]

    def far_step(p):
        block = blocks[p * 4]
        part[block] = combine(p * 4).astype(jnp.bfloat16)
        halves[p] = (
            links.start(
                part.at[block, pl.ds(0, half)], x_half.at[p, 0], hr[p], "seq", here.xr
            ),
            links.start(
                part.at[block, pl.ds(half, half)], x_half.at[p, 1], hl[p], "seq", here.xl
            ),
        )

    def near_step(p, side):
        order = p * 4 + 1 + side
        block = blocks[order]
        summed = combine(order)
        halves[p][side].wait_recv()
        arrived = x_half[p, side].astype(jnp.float32)
        low, high = summed[:half], summed[half:]
        if side == 0:
            low = low + arrived
        else:
            high = high + arrived
        part[block, pl.ds(0, half)] = low.astype(jnp.bfloat16)
        part[block, pl.ds(half, half)] = high.astype(jnp.bfloat16)
        fulls[p][side] = links.start(
            part.at[block],
            x_full.at[p, side],
            (fr if side == 0 else fl)[p],
            "seq",
            here.xr if side == 0 else here.xl,
        )

    def last_step(p):
        fulls[p][0].wait_recv()
        fulls[p][1].wait_recv()
        return x_full[p, 0].astype(jnp.float32) + x_full[p, 1].astype(jnp.float32)

    forward_y(0)
    forward_y(1)
    far_step(0)
    forward_y(2)
    near_step(0, 0)
    forward_y(3)
    near_step(0, 1)
    forward_y(4)
    part[blocks[3]] = combine(3).astype(jnp.bfloat16)
    forward_y(5)
    far_step(1)
    forward_y(6)
    part[blocks[3]] = (part[blocks[3]].astype(jnp.float32) + last_step(0)).astype(jnp.bfloat16)
    zc = links.start(part.at[blocks[3]], z_buf, z_id, "seq", here.zp)
    forward_y(7)
    near_step(1, 0)
    near_step(1, 1)
    total[...] = combine(7)
    total[...] = total[...] + last_step(1)
    zc.wait_recv()
    total[...] = total[...] + z_buf[...].astype(jnp.float32)
    if forward:
        gathered = grad_part[7]
        for copy in grads_sent:
            copy.wait_recv()
        for order in range(7):
            gathered = gathered + grad_got[order]
        gate_sum[...] = gathered
    links.finish()


COLLECT_SEMS = 1 + 8 + 40 + 16


def collect_scratch(forward):
    scratch = [
        pltpu.VMEM((4, 2, 8, CAP, WIDTH), jnp.bfloat16),
        pltpu.VMEM((8, LEN, WIDTH), jnp.bfloat16),
        pltpu.VMEM((8, 2, CAP, WIDTH), jnp.bfloat16),
        pltpu.VMEM((2, 2, LEN // 2, WIDTH), jnp.bfloat16),
        pltpu.VMEM((2, 2, LEN, WIDTH), jnp.bfloat16),
        pltpu.VMEM((LEN, WIDTH), jnp.bfloat16),
    ]
    if forward:
        scratch += [pltpu.VMEM((8, 8, LEN), jnp.float32), pltpu.VMEM((7, 8, LEN), jnp.float32)]
    return scratch + [
        pltpu.SemaphoreType.DMA((COLLECT_SEMS,)),
        pltpu.SemaphoreType.DMA((COLLECT_SEMS,)),
    ]


def collect_forward(results, table, gates, tokens):
    return pl.pallas_call(
        functools.partial(collect_kernel, True),
        name="collect_forward",
        out_shape=(
            jax.ShapeDtypeStruct((LEN, WIDTH), jnp.float32),
            jax.ShapeDtypeStruct((8, 8, LEN), jnp.float32),
            jax.ShapeDtypeStruct((8, LEN), jnp.float32),
        ),
        in_specs=[ANY, VMEM, VMEM, VMEM],
        out_specs=(VMEM, VMEM, VMEM),
        scratch_shapes=collect_scratch(True),
        compiler_params=params(3),
    )(results, table, gates, tokens)


def collect_backward(results, table, gates_all):
    return pl.pallas_call(
        functools.partial(collect_kernel, False),
        name="collect_backward",
        out_shape=jax.ShapeDtypeStruct((LEN, WIDTH), jnp.float32),
        in_specs=[ANY, VMEM, VMEM],
        out_specs=VMEM,
        scratch_shapes=collect_scratch(False),
        compiler_params=params(4),
    )(results, table, gates_all)


def small_sum_kernel(part, total, got, send, recv):
    me = lax.axis_index("grp")
    links = Links(send, recv)
    peers = [(me + shift) % 8 for shift in range(1, 8)]
    ids = links.ids(7)
    greet("grp", peers)
    copies = [
        links.start(part, got.at[me], ids[i], "grp", peers[i]) for i in range(7)
    ]
    got[me] = part[...]
    for copy in copies:
        copy.wait_recv()
    summed = got[0]
    for i in range(1, 8):
        summed = summed + got[i]
    total[...] = summed
    links.finish()


def small_sum(part, collective_id, name):
    shape = part.shape
    return pl.pallas_call(
        small_sum_kernel,
        name=name,
        out_shape=jax.ShapeDtypeStruct(shape, jnp.float32),
        in_specs=[VMEM],
        out_specs=VMEM,
        scratch_shapes=[
            pltpu.VMEM((8,) + shape, jnp.float32),
            pltpu.SemaphoreType.DMA((7,)),
            pltpu.SemaphoreType.DMA((7,)),
        ],
        compiler_params=params(collective_id),
    )(part)


CHUNK = 32
CHUNKS = 256 // CHUNK


def hidden_kernel(part, total, held, sibling, arrived, send, recv):
    me = lax.axis_index("grp")
    core, chip = me % 2, me // 2
    high = chip // 2
    depth = chip + high * (3 - 2 * chip)
    twin = chip * 2 + 1 - core
    inner = me + 2 - 4 * high
    outer = (me + 6 + 4 * high) % 8
    links = Links(send, recv)
    pair_id, chain_id, spread_id, share_id = (links.ids(2 * CHUNKS) for _ in range(4))
    outgoing, incoming = 1 - high, high
    barrier = pltpu.get_barrier_semaphore()
    for peer in (twin, inner):
        pl.semaphore_signal(barrier, inc=1, device_id={"grp": peer}, device_id_type=MESH)

    @pl.when(depth == 1)
    def _():
        pl.semaphore_signal(barrier, inc=1, device_id={"grp": outer}, device_id_type=MESH)
        pl.semaphore_wait(barrier, 3)

    @pl.when(depth == 0)
    def _():
        pl.semaphore_wait(barrier, 2)

    def local(stream, i):
        return pl.ds(pl.multiple_of(stream * 256 + i * CHUNK, CHUNK), CHUNK)

    def whole(half, stream, i):
        return pl.ds(pl.multiple_of(half * 512 + stream * 256 + i * CHUNK, CHUNK), CHUNK)

    def pair(stream, i):
        return links.copy(
            part.at[whole(1 - core, stream, i)],
            sibling.at[local(stream, i)],
            pair_id[0] + stream * CHUNKS + i,
            "grp",
            twin,
        )

    def chain(stream, i, peer):
        spot = local(stream, i)
        return links.copy(
            held.at[spot], arrived.at[spot], chain_id[0] + stream * CHUNKS + i, "grp", peer
        )

    def spread(stream, i, peer):
        spot = total.at[whole(core, stream, i)]
        return links.copy(spot, spot, spread_id[0] + stream * CHUNKS + i, "grp", peer)

    def share(stream, i):
        spot = total.at[whole(core, stream, i)]
        return links.copy(spot, spot, share_id[0] + stream * CHUNKS + i, "grp", twin)

    for i in range(CHUNKS):
        pair(outgoing, i).start()
        pair(incoming, i).start()

    def own_sum(stream, i):
        pair(stream, i).wait_recv()
        return part[whole(core, stream, i)].astype(jnp.float32) + sibling[
            local(stream, i)
        ].astype(jnp.float32)

    @pl.when(depth == 0)
    def _():
        for i in range(CHUNKS):
            held[local(outgoing, i)] = own_sum(outgoing, i).astype(jnp.bfloat16)
            chain(outgoing, i, inner).start()
        for i in range(CHUNKS):
            own = own_sum(incoming, i)
            chain(incoming, i, inner).wait_recv()
            total[whole(core, incoming, i)] = (
                own + arrived[local(incoming, i)].astype(jnp.float32)
            ).astype(jnp.bfloat16)
            spread(incoming, i, inner).start()
            share(incoming, i).start()
        for i in range(CHUNKS):
            spread(outgoing, i, inner).wait_recv()
            share(outgoing, i).start()
        for i in range(CHUNKS):
            chain(outgoing, i, inner).wait_send()
            spread(incoming, i, inner).wait_send()

    @pl.when(depth == 1)
    def _():
        def pass_on(stream, i, source, target):
            own = own_sum(stream, i)
            chain(stream, i, source).wait_recv()
            held[local(stream, i)] = (
                own + arrived[local(stream, i)].astype(jnp.float32)
            ).astype(jnp.bfloat16)
            chain(stream, i, target).start()

        def hand_out(stream, i, source, target):
            spread(stream, i, source).wait_recv()
            spread(stream, i, target).start()
            share(stream, i).start()

        for i in range(CHUNKS):
            pass_on(outgoing, i, outer, inner)
            pass_on(incoming, i, inner, outer)
        for i in range(CHUNKS):
            hand_out(incoming, i, outer, inner)
            hand_out(outgoing, i, inner, outer)
        for i in range(CHUNKS):
            chain(outgoing, i, inner).wait_send()
            chain(incoming, i, outer).wait_send()
            spread(incoming, i, inner).wait_send()
            spread(outgoing, i, outer).wait_send()

    for i in range(CHUNKS):
        for stream in (0, 1):
            pair(stream, i).wait_send()
            share(stream, i).wait()


def hidden_sum(part):
    sems = 8 * CHUNKS
    return pl.pallas_call(
        hidden_kernel,
        name="hidden_sum",
        out_shape=jax.ShapeDtypeStruct((1024, FF), jnp.bfloat16),
        in_specs=[VMEM],
        out_specs=VMEM,
        scratch_shapes=[
            pltpu.VMEM((512, FF), jnp.bfloat16),
            pltpu.VMEM((512, FF), jnp.bfloat16),
            pltpu.VMEM((512, FF), jnp.bfloat16),
            pltpu.SemaphoreType.DMA((sems,)),
            pltpu.SemaphoreType.DMA((sems,)),
        ],
        compiler_params=params(5),
    )(part)


KEYS = 512


def attend_kernel(bounds, query, kv, first_key, query_pos, inputs, resid, best, total, acc):
    scale = HEAD_DIM ** (-0.5) * 1.4426950408889634
    groups = HEADS // KV_HEADS
    best[...] = jnp.full(best.shape, -1e30, jnp.float32)
    total[...] = jnp.zeros(total.shape, jnp.float32)
    acc[...] = jnp.zeros(acc.shape, jnp.float32)

    def step(i, carry):
        start = pl.multiple_of(i * KEYS, KEYS)
        keys = kv[pl.ds(start, KEYS), pl.ds(0, HEAD_DIM)]
        values = kv[pl.ds(start, KEYS), pl.ds(HEAD_DIM, HEAD_DIM)]
        key_pos = start + lax.broadcasted_iota(jnp.int32, (LEN, KEYS), 1)
        allowed = (key_pos <= query_pos[...]) & (key_pos >= first_key[...])
        for h in range(groups):
            scores = lax.dot_general(
                query[:, h * HEAD_DIM : (h + 1) * HEAD_DIM],
                keys,
                (((1,), (1,)), ((), ())),
                preferred_element_type=jnp.float32,
            )
            scores = jnp.where(allowed, scores, -1e30)
            old = best[h]
            new = jnp.maximum(old, jnp.max(scores, axis=1, keepdims=True))
            weights = jnp.where(allowed, jnp.exp2((scores - new) * scale), 0.0)
            shrink = jnp.exp2((old - new) * scale)
            best[h] = new
            total[h] = total[h] * shrink + jnp.sum(weights, axis=1, keepdims=True)
            acc[h] = acc[h] * shrink + jnp.dot(
                weights.astype(jnp.bfloat16), values, preferred_element_type=jnp.float32
            )
        return carry

    lax.fori_loop(bounds[0], bounds[1], step, 0)
    for h in range(groups):
        cols = slice(h * HEAD_DIM, (h + 1) * HEAD_DIM)
        attended = (acc[h] / total[h]).astype(jnp.bfloat16).astype(jnp.float32)
        resid[:, cols] = (inputs[:, cols].astype(jnp.float32) + attended).astype(jnp.bfloat16)


def attend(query, kv, doc_ids, inputs):
    first_query = lax.axis_index("seq") * LEN
    query_pos = first_query + jnp.arange(LEN, dtype=jnp.int32)
    query_doc = lax.dynamic_slice_in_dim(doc_ids, first_query, LEN)
    first_key = jnp.sum(
        (doc_ids[None, :] < query_doc[:, None]).astype(jnp.int32), axis=1, keepdims=True
    )
    bounds = jnp.stack([first_key[0, 0] // KEYS, (first_query + LEN + KEYS - 1) // KEYS])
    groups = HEADS // KV_HEADS
    return pl.pallas_call(
        attend_kernel,
        name="attend",
        out_shape=jax.ShapeDtypeStruct((LEN, WIDTH), jnp.bfloat16),
        in_specs=[pl.BlockSpec(memory_space=pltpu.SMEM)] + [VMEM] * 5,
        out_specs=VMEM,
        scratch_shapes=[
            pltpu.VMEM((groups, LEN, 1), jnp.float32),
            pltpu.VMEM((groups, LEN, 1), jnp.float32),
            pltpu.VMEM((groups, LEN, HEAD_DIM), jnp.float32),
        ],
        compiler_params=params(),
    )(bounds.astype(jnp.int32), query, kv, first_key, query_pos[:, None], inputs)


def gelu_slope(pre_act):
    return jax.vjp(lambda inner: jax.nn.gelu(inner, approximate=True), pre_act)[1](
        jnp.ones_like(pre_act)
    )[0]


def body(
    inputs,
    query_states,
    key_states,
    value_states,
    doc_ids,
    modality,
    expert_ids,
    norm_gain,
    router_w,
    w_in,
    w_out,
    grad_out,
):
    length, width = inputs.shape
    experts = lax.axis_size("seq")
    kept_mask = expert_ids >= 0
    kept_wide = kept_mask.astype(jnp.float32)
    column = modality[:, None] * experts + jnp.where(kept_mask, expert_ids, 0)
    one_hot = (
        column[:, :, None] == jnp.arange(2 * experts, dtype=jnp.int32)[None, None, :]
    ) & kept_mask[:, :, None]
    entries = length * TOP
    flat_hot = one_hot.reshape(entries, 2 * experts).astype(jnp.bfloat16)
    entry_range = jnp.arange(entries, dtype=jnp.int32)
    earlier = (entry_range[:, None] > entry_range[None, :]).astype(jnp.bfloat16)
    before = jnp.dot(earlier, flat_hot, preferred_element_type=jnp.float32)
    slot_rank = jnp.sum(before * flat_hot.astype(jnp.float32), axis=1).astype(jnp.int32)
    slots = jnp.where(kept_mask, column * CAP + slot_rank.reshape(length, TOP), -1)
    slots = jnp.concatenate([slots.T, jnp.full((8 - TOP, length), -1, jnp.int32)], axis=0)

    w_in_local = w_in[:, 0]
    w_out_local = w_out[:, 0]

    got_grads, tokens_grad, table = dispatch_first(grad_out, slots)
    partial_back = jnp.einsum(
        "ukx,utx->ukt",
        got_grads.reshape(2, experts * CAP, width),
        w_out_local,
        preferred_element_type=jnp.float32,
    ).astype(jnp.bfloat16)
    act_grad = lax.psum(partial_back, "grp")

    kv = gather_kv(jnp.concatenate([key_states, value_states], axis=1))
    resid_state = attend(query_states, kv.reshape(experts * length, 2 * HEAD_DIM), doc_ids, inputs)
    state_wide = resid_state.astype(jnp.float32)
    scaled = state_wide * norm_gain[None, :]
    raw_part = lax.dot_general(
        router_w,
        scaled.astype(jnp.bfloat16),
        (((0,), (1,)), ((), ())),
        preferred_element_type=jnp.float32,
    )
    square_part = jnp.sum(state_wide * state_wide, axis=1)[None, :]
    stats = small_sum(
        jnp.concatenate([raw_part, square_part, jnp.zeros((7, length), jnp.float32)], axis=0),
        6,
        "sum_stats",
    )
    inv_row = lax.rsqrt(stats[2 * experts] / D + eps_norm)
    inv_rms = inv_row[:, None]
    raw_logits = stats[: 2 * experts].T
    logits = raw_logits * inv_rms
    normed = (scaled * inv_rms).astype(jnp.bfloat16)
    chosen = jnp.sum(jnp.where(one_hot, logits[:, None, :], 0.0), axis=2)
    lifted = jax.nn.sigmoid(chosen)
    denominator = gate_offset + jnp.sum(kept_wide * lifted, axis=1, keepdims=True)
    gates = kept_wide * lifted / denominator
    gates_t = jnp.concatenate([gates.T, jnp.zeros((8 - TOP, length), jnp.float32)], axis=0)

    got_rows = dispatch_next(normed, table)
    partial_value = jnp.einsum(
        "ohn,ons->ohs",
        got_rows.reshape(2, experts * CAP, width),
        w_in_local,
        preferred_element_type=jnp.float32,
    ).astype(jnp.bfloat16)
    pre_act = hidden_sum(partial_value.reshape(2 * experts * CAP, FF)).reshape(
        2, experts * CAP, FF
    )
    pre_wide = pre_act.astype(jnp.float32)
    active = jax.nn.gelu(pre_wide, approximate=True).astype(jnp.bfloat16)
    expert_out = jnp.einsum(
        "nuv,nvg->nug", active, w_out_local, preferred_element_type=jnp.float32
    ).astype(jnp.bfloat16)
    mixture, gates_all, gate_part = collect_forward(
        expert_out.reshape(2, 4, 8, CAP, width), table, gates_t, tokens_grad
    )
    layer_out = (state_wide + mixture).astype(jnp.bfloat16)

    pre_grad = (gelu_slope(pre_wide) * act_grad.astype(jnp.float32)).astype(jnp.bfloat16)
    entry_grad = jnp.einsum(
        "upj,uoj->upo", pre_grad, w_in_local, preferred_element_type=jnp.float32
    ).astype(jnp.bfloat16)
    entry_sum = collect_backward(entry_grad.reshape(2, 4, 8, CAP, width), table, gates_all)
    entry_dot = jnp.sum(entry_sum * scaled, axis=1)[None, :]
    row_index = jnp.arange(8, dtype=jnp.int32)[:, None]
    ends = small_sum(jnp.where(row_index == TOP, entry_dot, gate_part), 7, "sum_ends")
    gate_grad = ends[:TOP].T
    gate_dot = jnp.sum(gates * gate_grad, axis=1, keepdims=True)
    logit_grad = kept_wide * (gate_grad - gate_dot) / denominator * lifted * (1.0 - lifted)
    logit_full = jnp.sum(jnp.where(one_hot, logit_grad[:, :, None], 0.0), axis=1)
    router_grad = jnp.dot(
        logit_full, router_w.astype(jnp.float32).T, precision=lax.Precision.HIGHEST
    )
    norm_dot = ends[TOP][:, None] + jnp.sum(logit_full * raw_logits, axis=1, keepdims=True)
    normed_grad = router_grad + entry_sum
    state_grad = (
        grad_out.astype(jnp.float32)
        + inv_rms * norm_gain[None, :] * normed_grad
        - inv_rms**3 / D * state_wide * norm_dot
    )
    return (layer_out, state_grad.astype(jnp.bfloat16))


def solution(mesh):
    in_specs = (
        P("seq", "grp"),
        P("seq", "grp"),
        P("seq", "grp"),
        P("seq", "grp"),
        P(),
        P("seq"),
        P("seq", None),
        P("grp"),
        P("grp", None),
        P(None, "seq", "grp", None),
        P(None, "seq", None, "grp"),
        P("seq", "grp"),
    )
    out_specs = (P("seq", "grp"), P("seq", "grp"))
    return jax.shard_map(body, mesh=mesh, in_specs=in_specs, out_specs=out_specs, check_vma=False)
```

time: 652 us -> 422 us (0.65)
  waiting for transfers between devices: 413 us -> 0.02 us
  Pallas kernels: 0 us -> 349 us
  blocking collectives: 104 us -> 0 us
  starting transfers between devices: 33.5 us -> 0.04 us
  local copies, waits for them, and re-layouts: 20.5 us -> 2.84 us
  matrix products: 48.5 us -> 40.4 us
    pallas_call x0 -> x9, Pallas kernels: none -> 349 us  [the longest x1 83.3 us: hidden_sum(): pl.pallas_call(hidden_kernel, name='hidden_sum', out_shape=jax.ShapeDtype...]
    all_gather x2 -> x0, waiting for transfers between devices: 148 us -> none  [the longest x1 79.9 us: attend(): key_piece = lax.all_gather(key_states, 'seq', axis=0, tiled=True)]
    psum x1, waiting for transfers between devices: 136 us -> 0.01 us  [body(): act_grad = lax.psum(partial_back, 'grp')]
    all_to_all x4 -> x0, waiting for transfers between devices: 128 us -> none  [the longest x2 88.4 us: dispatch(): lax.all_to_all(buffers, 'seq', split_axis=1, concat_axis=1, tiled=True)]
    psum x4 -> x0, blocking collectives: 104 us -> none  [row_total(): return lax.psum(partial_value, 'grp')]
    all_to_all x4 -> x0, starting transfers between devices: 33.4 us -> none  [the longest x2 18.6 us: collect(): lax.all_to_all(buffers, 'seq', split_axis=1, concat_axis=1, tiled=True)]
    dot_general x12 -> x5, matrix products: 47.6 us -> 37.9 us  [the longest x1 11.1 us: body(): jnp.einsum('upj,uoj->upo', pre_grad, w_in_local, preferred_element_type=j...]
    unnamed x21 -> x36, local copies, waits for them, and re-layouts: 8.51 us -> 0.08 us
  transfers between devices with their start and end apart: 7 -> 1, of which waited for: 6 -> 0; matrix products, arithmetic and copies ran while one was open for 6% -> 7% of each run, Pallas kernels for 0% -> 58%
where the time goes in v1:
time: 422 us; the launch traced here: 421 us
  Pallas kernels  349 us (83%)
  matrix products  40.4 us (10%)
  between operations  14.5 us (3%)
  other arithmetic  13.7 us (3%)
    pallas_call x1, Pallas kernels, hidden_sum(): pl.pallas_call(hidden_kernel, name='hidden_sum', out_shape=jax.ShapeDtype...  83.3 us
    pallas_call x1, Pallas kernels, dispatch_next(): pl.pallas_call(functools.partial(dispatch_kernel, False), name='dispatch_...  60.7 us
    pallas_call x1, Pallas kernels, collect_forward(): pl.pallas_call(functools.partial(collect_kernel, True), name='collect_for...  50.5 us
    pallas_call x1, Pallas kernels, dispatch_first(): pl.pallas_call(functools.partial(dispatch_kernel, True), name='dispatch_g...  46.6 us
    pallas_call x1, Pallas kernels, collect_backward(): pl.pallas_call(functools.partial(collect_kernel, False), name='collect_ba...  44 us
    pallas_call x2, Pallas kernels, small_sum(): pl.pallas_call(small_sum_kernel, name=name, out_shape=jax.ShapeDtypeStruc...  31.8 us
    pallas_call x1, Pallas kernels, gather_kv(): pl.pallas_call(kv_kernel, name='gather_kv', out_shape=jax.ShapeDtypeStruc...  26.8 us
    dot_general x1, matrix products, body(): jnp.einsum('upj,uoj->upo', pre_grad, w_in_local, preferred_element_type=j...  11.1 us
  transfers between devices with their start and end apart: 1, of which 0 were waited for; matrix products, arithmetic and copies ran while one was open for 7% of the time, Pallas kernels for 58%

profile of v1, /device:TPU:1, one launch (start us, length us, event | category | flops | bytes accessed | tf_op | source)
XLA Modules:
  0.0 421.0 jit_solution(2937231826027667525)
XLA Ops:
  7.2 0.0 copy-start
  7.2 0.0 all-reduce.4.cloned.1.call-start
  7.2 0.7 broadcast_multiply_fusion
  7.9 0.7 select_add_fusion
  8.6 0.1 copy.29
  8.7 0.1 and.27
  8.9 0.1 copy.28
  9.0 0.1 eq.30
  9.1 0.3 fusion.50
  9.4 0.1 convert_element_type.71
  9.5 0.1 copy.30
  9.6 0.6 concatenate.14.refs_1_
  10.2 46.6 %dispatch_grads.1 = (bf16[2,4,8,16,1024]{4,3,2,1,0:T(8,128)(2,1)}, bf16[8,128,1024]{2,1,0:T(8,128)(2,1)}, s32[8,8,128]{2,1,0:T(8,128)}) custom-call(bf16[128,1024]{1,0:T(8,128)(2,1)} %refs_0_.1, s32[8,128]{1,0:T(8,128)} %concatenate.14.refs_1_), custom_call_target="tpu_custom_call" | custom-call | tf_op jit(solution)/shard_map/dispatch_grads/pallas_call | solution.py:358
  56.8 0.0 copy-start.10
  56.8 0.0 copy-start.8
  56.8 0.0 copy-start.9
  56.8 8.4 %fusion.21 = bf16[2,512,1408]{2,1,0:T(8,128)(2,1)} fusion(bf16[2,512,1024]{2,1,0:T(8,128)(2,1)} %bitcast.75, bf16[2,1,1408,1024]{3,2,1,0:T(8,128)(2,1)} %param.22), kind=kOutput, calls=%fused_computation.24 | convolution fusion | flops 2954231808 | bytes 10747904 | tf_op jit(solution)/shard_map/ukx,utx->ukt/dot_general | solution.py:905
  65.2 0.0 all-reduce.4.cloned.1.call-update
  65.2 0.0 copy-done.10
  65.2 0.1 dynamic_slice.3
  65.3 0.4 convert_reduce_fusion
  65.8 0.6 iota_add_fusion.query_pos
  66.5 0.7 copy.27.first_key
  67.2 0.0 copy-done.8
  67.2 0.0 copy-done.9
  67.2 0.6 pad_maximum_fusion.kv_in
  67.8 26.8 %gather_kv.1 = bf16[32,128,256]{2,1,0:T(8,128)(2,1)} custom-call(bf16[128,256]{1,0:T(8,128)(2,1)} %pad_maximum_fusion.kv_in), custom_call_target="tpu_custom_call" | custom-call | tf_op jit(solution)/shard_map/gather_kv/pallas_call | solution.py:199
  94.7 0.6 pad_add_fusion.bounds
  95.3 5.9 %attend.1 = bf16[128,1024]{1,0:T(8,128)(2,1)} custom-call(s32[2]{0:T(128)} %pad_add_fusion.bounds, bf16[128,1024]{1,0:T(8,128)(2,1)} %query.1, bf16[4096,256]{1,0:T(8,128)(2,1)} %bitcast.62, s32[128,1]{1,0:T(8,128)} %copy.27.first_key, s32[128,1]{1,0:T(8,128)} %iota_add_fusion.query_pos, bf16[128,1024]{1,0:T(8,128)(2,1)} %inputs.1), custom_call_target="tpu_custom_call" | custom-call | tf_op jit(solution)/shard_map/attend/pallas_call | solution.py:849
  101.1 1.1 fusion.56
  102.2 0.0 copy-done
  102.2 0.0 copy-done.7
  102.2 1.2 convolution_bitcast_fusion
  103.4 0.1 pad.4.clone
  103.5 0.7 maximum_maximum_fusion.part
  104.2 17.8 %sum_stats.1 = f32[72,128]{1,0:T(8,128)} custom-call(f32[72,128]{1,0:T(8,128)} %maximum_maximum_fusion.part), custom_call_target="tpu_custom_call" | custom-call | tf_op jit(solution)/shard_map/sum_stats/pallas_call | solution.py:644
  122.0 1.3 fusion.72
  123.3 1.8 fusion.54.refs_0_
  125.0 60.7 %dispatch_rows.1 = bf16[2,4,8,16,1024]{4,3,2,1,0:T(8,128)(2,1)} custom-call(bf16[128,1024]{1,0:T(8,128)(2,1)} %fusion.54.refs_0_, s32[8,8,128]{2,1,0:T(8,128)} %get-tuple-element.8.refs_1_), custom_call_target="tpu_custom_call" | custom-call | tf_op jit(solution)/shard_map/dispatch_rows/pallas_call | solution.py:379
  185.7 8.4 %fusion.18 = bf16[2,512,1408]{2,1,0:T(8,128)(2,1)} fusion(bf16[2,512,1024]{2,1,0:T(8,128)(2,1)} %bitcast.67, bf16[2,1,1024,1408]{3,2,1,0:T(8,128)(2,1)} %param.21), kind=kOutput, calls=%fused_computation.23 | convolution fusion | flops 2954231808 | bytes 10747904 | tf_op jit(solution)/shard_map/ohn,ons->ohs/dot_general | solution.py:941
  194.1 83.3 %hidden_sum.1 = bf16[1024,1408]{1,0:T(8,128)(2,1)} custom-call(bf16[1024,1408]{1,0:T(8,128)(2,1)} %bitcast.65), custom_call_target="tpu_custom_call" | custom-call | tf_op jit(solution)/shard_map/hidden_sum/pallas_call | solution.py:781
  277.3 0.0 copy-done.11
  277.3 0.0 copy-done.5
  277.5 0.6 concatenate.15.refs_2_
  278.1 0.0 copy-done.13
  278.1 8.9 %fusion.36 = bf16[2,512,1024]{2,1,0:T(8,128)(2,1)} fusion(bf16[2,1,1408,1024]{3,2,1,0:T(8,128)(2,1)} %param.22, bf16[2,512,1408]{2,1,0:T(8,128)(2,1)} %bitcast.63), kind=kOutput, calls=%fused_computation.36 | convolution fusion | flops 2968256512 | bytes 10747904 | tf_op jit(solution)/shard_map/nuv,nvg->nug/dot_general | solution.py:952
  287.0 50.5 %collect_forward.1 = (f32[128,1024]{1,0:T(8,128)}, f32[8,8,128]{2,1,0:T(8,128)}, f32[8,128]{1,0:T(8,128)}) custom-call(bf16[2,4,8,16,1024]{4,3,2,1,0:T(8,128)(2,1)} %bitcast.66, s32[8,8,128]{2,1,0:T(8,128)} %get-tuple-element.8.refs_1_, f32[8,128]{1,0:T(8,128)} %concatenate.15.refs_2_, bf16[8,128,1024]{2,1,0:T(8,128)(2,1)} %get-tuple-element.9.refs_3_), custom_call_target="tpu_custom_call" | custom-call | tf_op jit(solution)/shard_map/collect_forward/pallas_call | solution.py:596
  337.4 0.5 iota_compare_fusion.4
  338.0 0.0 copy-done.2
  338.0 0.0 copy-start.4
  338.0 0.0 copy-start.15
  338.0 0.0 copy-start.17
  338.0 0.0 copy-start.14
  338.1 11.1 %fusion.41 = bf16[2,512,1024]{2,1,0:T(8,128)(2,1)} fusion(bf16[2,1,1024,1408]{3,2,1,0:T(8,128)(2,1)} %param.21, bf16[2,512,1408]{2,1,0:T(8,128)(2,1)S(1)} %bitcast.64, bf16[2,512,1408]{2,1,0:T(8,128)(2,1)} %all-reduce.4.cloned.1.call-done), kind=kOutput, calls=%fused_computation.37 | convolution fusion | flops 2984116224 | bytes 13631488 | tf_op jit(solution)/shard_map/upj,uoj->upo/dot_general | solution.py:961
  349.1 44.0 %collect_backward.1 = f32[128,1024]{1,0:T(8,128)} custom-call(bf16[2,4,8,16,1024]{4,3,2,1,0:T(8,128)(2,1)} %bitcast.68, s32[8,8,128]{2,1,0:T(8,128)} %get-tuple-element.8.refs_1_, f32[8,8,128]{2,1,0:T(8,128)} %get-tuple-element.12.refs_2_), custom_call_target="tpu_custom_call" | custom-call | tf_op jit(solution)/shard_map/collect_backward/pallas_call | solution.py:612
  393.2 1.9 fusion.55
  395.0 0.0 copy-done.15
  395.0 0.7 broadcast_select_fusion.part
  395.7 14.0 %sum_ends.1 = f32[8,128]{1,0:T(8,128)} custom-call(f32[8,128]{1,0:T(8,128)} %broadcast_select_fusion.part), custom_call_target="tpu_custom_call" | custom-call | tf_op jit(solution)/shard_map/sum_ends/pallas_call | solution.py:644
  409.7 0.7 fusion.69
  410.4 0.7 fusion.68
  411.2 0.7 bitcast_add_fusion
  411.9 0.0 copy-done.12
  411.9 2.3 fusion.49
  (28 shorter events, 0.2 us)
Async XLA Ops:
  7.2 95.1 %copy-start = (bf16[1024,64]{0,1:T(8,128)(2,1)S(1)}, bf16[1024,64]{0,1:T(8,128)(2,1)}, u32[]{:S(2)}) copy-start(bf16[1024,64]{0,1:T(8,128)(2,1)} %param.20) | copy-start | bytes 393220
  7.2 330.8 %all-reduce.4.cloned.1.call-start = ((), (), s32[]{:S(2)}) async-start(), calls=%async_computation | async-start | bytes 5767168 | tf_op jit(solution)/shard_map/psum | solution.py:911
  56.8 8.4 %copy-start.10 = (s32[4096]{0:T(1024)S(1)}, s32[4096]{0:T(1024)}, u32[]{:S(2)}) copy-start(s32[4096]{0:T(1024)} %param.16) | copy-start | bytes 49156
  56.8 10.4 %copy-start.8 = (bf16[128,128]{1,0:T(8,128)(2,1)S(1)}, bf16[128,128]{1,0:T(8,128)(2,1)}, u32[]{:S(2)}) copy-start(bf16[128,128]{1,0:T(8,128)(2,1)} %param.15) | copy-start | bytes 98308
  56.8 10.4 %copy-start.9 = (bf16[128,128]{1,0:T(8,128)(2,1)S(1)}, bf16[128,128]{1,0:T(8,128)(2,1)}, u32[]{:S(2)}) copy-start(bf16[128,128]{1,0:T(8,128)(2,1)} %param.14) | copy-start | bytes 98308
  65.2 37.0 %copy-start.7 = (f32[1024]{0:T(1024)S(1)}, f32[1024]{0:T(1024)}, u32[]{:S(2)}) copy-start(f32[1024]{0:T(1024)} %param.19) | copy-start | bytes 12292
  123.3 154.1 %copy-start.11 = (f32[128]{0:T(128)}, f32[128]{0:T(128)S(1)}, u32[]{:S(2)}) copy-start(f32[128]{0:T(128)S(1)} %get-tuple-element.15) | copy-start | bytes 1540
  194.0 83.3 %copy-start.5 = (f32[72,128]{1,0:T(8,128)S(1)}, f32[72,128]{1,0:T(8,128)}, u32[]{:S(2)}) copy-start(f32[72,128]{1,0:T(8,128)} %sum_stats.1) | copy-start | bytes 110596
  277.4 0.6 copy-start.13
  278.1 59.9 %copy-start.2 = (bf16[1024,1408]{1,0:T(8,128)(2,1)S(1)}, bf16[1024,1408]{1,0:T(8,128)(2,1)}, u32[]{:S(2)}) copy-start(bf16[1024,1408]{1,0:T(8,128)(2,1)} %hidden_sum.1) | copy-start | bytes 8650756
  338.0 55.2 %copy-start.1 = (bf16[128,1024]{1,0:T(8,128)(2,1)S(1)}, bf16[128,1024]{1,0:T(8,128)(2,1)}, u32[]{:S(2)}) copy-start(bf16[128,1024]{1,0:T(8,128)(2,1)} %attend.1) | copy-start | bytes 786436
  338.0 73.9 %copy-start.3 = (bf16[128,1024]{1,0:T(8,128)(2,1)S(1)}, bf16[128,1024]{1,0:T(8,128)(2,1)}, u32[]{:S(2)}) copy-start(bf16[128,1024]{1,0:T(8,128)(2,1)} %refs_0_.1) | copy-start | bytes 786436
  338.0 55.2 %copy-start.4 = (f32[128,1024]{1,0:T(8,128)S(1)}, f32[128,1024]{1,0:T(8,128)}, u32[]{:S(2)}) copy-start(f32[128,1024]{1,0:T(8,128)} %get-tuple-element.10) | copy-start | bytes 1572868
  338.0 57.0 %copy-start.15 = (f32[8,128]{1,0:T(8,128)S(1)}, f32[8,128]{1,0:T(8,128)}, u32[]{:S(2)}) copy-start(f32[8,128]{1,0:T(8,128)} %get-tuple-element.13) | copy-start | bytes 12292
  338.0 57.0 %copy-start.17 = (pred[8]{0:T(512)(128)(4,1)S(1)}, pred[8]{0:T(512)(128)(4,1)}, u32[]{:S(2)}) copy-start(pred[8]{0:T(512)(128)(4,1)} %iota_compare_fusion.4) | copy-start | bytes 28
  338.0 71.7 %copy-start.14 = (f32[128]{0:T(128)S(1)}, f32[128]{0:T(128)}, u32[]{:S(2)}) copy-start(f32[128]{0:T(128)} %copy-done.13) | copy-start | bytes 1540
  338.0 73.1 %copy-start.6 = (f32[72,128]{1,0:T(8,128)S(1)}, f32[72,128]{1,0:T(8,128)}, u32[]{:S(2)}) copy-start(f32[72,128]{1,0:T(8,128)} %sum_stats.1) | copy-start | bytes 110596
  338.0 73.8 %copy-start.12 = (f32[128]{0:T(128)S(1)}, f32[128]{0:T(128)}, u32[]{:S(2)}) copy-start(f32[128]{0:T(128)} %copy-done.11) | copy-start | bytes 1540
  338.0 73.8 %copy-start.16 = (f32[128]{0:T(128)S(1)}, f32[128]{0:T(128)}, u32[]{:S(2)}) copy-start(f32[128]{0:T(128)} %get-tuple-element.14) | copy-start | bytes 1540
Sparse Core Ops, SparseCore 0:
  65.3 105.9 all-reduce.3

commit v2 on v0

v2 whole, which is shorter than its diff:
```python
import functools

import jax
import jax.numpy as jnp
from jax import lax
from jax.experimental import pallas as pl
from jax.experimental.pallas import tpu as pltpu
from jax.sharding import PartitionSpec as P

D = 8192
HEADS = 64
KV_HEADS = 8
HEAD_DIM = 128
FF = 1408
TOP = 4
CAP = 16
LEN = 128
WIDTH = 1024

eps_norm = 1e-05
gate_offset = 0.5

MESH = pl.DeviceIdType.MESH
VMEM = pl.BlockSpec(memory_space=pltpu.VMEM)
ANY = pl.BlockSpec(memory_space=pl.ANY)
LIMIT = 56 * 1024 * 1024


def params(collective_id=None):
    if collective_id is None:
        return pltpu.CompilerParams(vmem_limit_bytes=LIMIT)
    return pltpu.CompilerParams(
        collective_id=collective_id, has_side_effects=True, vmem_limit_bytes=LIMIT
    )


class Links:
    def __init__(self, send, recv):
        self.send, self.recv = send, recv
        self.used = 0
        self.started = []

    def ids(self, count):
        first = self.used
        self.used += count
        return [first + i for i in range(count)]

    def copy(self, src, dst, index, axis, peer):
        return pltpu.make_async_remote_copy(
            src_ref=src,
            dst_ref=dst,
            send_sem=self.send.at[index],
            recv_sem=self.recv.at[index],
            device_id={axis: peer},
            device_id_type=MESH,
        )

    def start(self, src, dst, index, axis, peer):
        copy = self.copy(src, dst, index, axis, peer)
        copy.start()
        self.started.append(copy)
        return copy

    def local(self, src, dst, index):
        copy = pltpu.make_async_copy(src, dst, self.send.at[index])
        copy.start()
        return copy

    def finish(self):
        for copy in self.started:
            copy.wait_send()


def greet(axis, peers):
    barrier = pltpu.get_barrier_semaphore()
    for peer in peers:
        pl.semaphore_signal(barrier, inc=1, device_id={axis: peer}, device_id_type=MESH)
    pl.semaphore_wait(barrier, len(peers))


class Flow:
    def __init__(self, which, half):
        me = lax.axis_index("seq")
        y, z, x = me // 8, (me % 8) // 4, me % 4
        self.me, self.z, self.which = me, z, which
        if which == 0:
            self.a, self.b, self.step_a, self.step_b = x, y, 1, 8
        else:
            self.a, self.b, self.step_a, self.step_b = y, x, 8, 1
        self.cols = pl.ds(which * half, half)
        self.home = z * 4 + self.a
        self.zp = self.at(z=1 - z)
        self.ar, self.al = self.at(da=1), self.at(da=3)
        self.br, self.bl = self.at(db=1), self.at(db=3)

    def at(self, z=None, da=0, db=0):
        z = self.z if z is None else z
        return z * 4 + ((self.a + da) % 4) * self.step_a + ((self.b + db) % 4) * self.step_b

    def row(self, db):
        return (self.b + db) % 4

    def block(self, z, da):
        return z * 4 + (self.a + da) % 4

    def codes(self):
        row = lax.broadcasted_iota(jnp.int32, (LEN, LEN), 0)
        owner = (row // 32) * self.step_b + self.z * 4 + self.a * self.step_a
        return (((row // 16) % 2) * 32 + owner) * CAP + row % 16

    def family(self):
        return [self.at(da=d) for d in (1, 2, 3)] + [
            self.at(z=1 - self.z, da=d) for d in (0, 1, 2, 3)
        ]


def near_peers(flow):
    return [flow.zp, flow.ar, flow.al, flow.br, flow.bl]


def all_peers(flow, other):
    return flow.family() + other.family()[:3] + other.family()[4:]


HALF = LEN // 2
SHIFTS = [0, 3, 1, 2]


class GatherStream:
    def __init__(self, links, flow, source, out):
        self.links, self.flow, self.out = links, flow, out
        self.source = source.at[:, flow.cols]
        self.zs = [flow.z, 1 - flow.z]
        self.own_id, self.z_id = links.ids(2)
        self.a1r, self.a1l, self.a2r, self.a2l = (links.ids(2) for _ in range(4))
        self.r_id, self.l_id, self.f_id = (links.ids(8) for _ in range(3))
        self.sent, self.first, self.second, self.far = {}, {}, {}, {}

    def spot(self, order, db=0, rows=None):
        flow = self.flow
        place = flow.at(z=self.zs[order // 4], da=SHIFTS[order % 4], db=db)
        rows = pl.ds(0, LEN) if rows is None else rows
        return self.out.at[place, rows, flow.cols]

    def piece(self, order):
        return self.source if order == 0 else self.spot(order)

    def begin(self):
        self.own = self.links.local(self.source, self.spot(0), self.own_id)
        self.zc = self.links.start(self.source, self.spot(0), self.z_id, "seq", self.flow.zp)
        self.send_a(0)

    def send_a(self, p):
        src, dst = self.piece(p * 4), self.spot(p * 4)
        self.first[p] = (
            self.links.start(src, dst, self.a1r[p], "seq", self.flow.ar),
            self.links.start(src, dst, self.a1l[p], "seq", self.flow.al),
        )

    def forward_a(self, p):
        low, high = pl.ds(0, HALF), pl.ds(HALF, HALF)
        self.first[p][0].wait_recv()
        left = self.spot(p * 4 + 1, rows=low)
        one = self.links.start(left, left, self.a2r[p], "seq", self.flow.ar)
        self.first[p][1].wait_recv()
        right = self.spot(p * 4 + 2, rows=high)
        two = self.links.start(right, right, self.a2l[p], "seq", self.flow.al)
        self.second[p] = (one, two)

    def far_a(self, p):
        self.second[p][0].wait_recv()
        self.second[p][1].wait_recv()

    def other_z(self):
        self.zc.wait_recv()
        self.send_a(1)

    def pick(self, order):
        src, dst = self.piece(order), self.spot(order)
        self.sent[order] = (
            self.links.start(src, dst, self.r_id[order], "seq", self.flow.br),
            self.links.start(src, dst, self.l_id[order], "seq", self.flow.bl),
        )

    def forward_b(self, order):
        right = order % 2 == 0
        self.sent[order][0 if right else 1].wait_recv()
        piece = self.spot(order, db=3 if right else 1)
        self.far[order] = self.links.start(
            piece, piece, self.f_id[order], "seq", self.flow.br if right else self.flow.bl
        )

    def finish(self):
        for order in range(8):
            self.sent[order][1 if order % 2 == 0 else 0].wait_recv()
            self.far[order].wait_recv()
        self.own.wait()


class DispatchStream:
    def __init__(self, links, flow, rows, tokens, table, out_buf, far_buf, got):
        k = flow.which
        self.links, self.flow, self.got = links, flow, got
        self.rows = rows.at[:, flow.cols]
        self.tokens, self.table = tokens.at[k], table.at[k]
        self.out_buf, self.far_buf = out_buf.at[k], far_buf.at[k]
        self.zs = [flow.z, 1 - flow.z]
        (self.z_id,) = links.ids(1)
        self.a1r, self.a1l, self.a2r, self.a2l = (links.ids(2) for _ in range(4))
        self.r_id, self.l_id, self.f1_id, self.f2_id, self.own_id = (
            links.ids(8) for _ in range(5)
        )
        self.sent, self.first, self.second, self.far, self.kept = {}, {}, {}, {}, []
        self.codes = flow.codes()

    def block(self, order):
        return self.flow.block(self.zs[order // 4], SHIFTS[order % 4])

    def begin(self):
        mine = self.tokens.at[self.flow.home]
        self.zc = self.links.start(self.rows, mine, self.z_id, "seq", self.flow.zp)
        self.send_a(0, self.rows)
        self.tokens[self.flow.home] = self.rows[...]

    def send_a(self, p, src=None):
        spot = self.tokens.at[self.block(p * 4)]
        src = spot if src is None else src
        self.first[p] = (
            self.links.start(src, spot, self.a1r[p], "seq", self.flow.ar),
            self.links.start(src, spot, self.a1l[p], "seq", self.flow.al),
        )

    def forward_a(self, p):
        self.first[p][0].wait_recv()
        left = self.tokens.at[self.block(p * 4 + 1), pl.ds(0, HALF)]
        one = self.links.start(left, left, self.a2r[p], "seq", self.flow.ar)
        self.first[p][1].wait_recv()
        right = self.tokens.at[self.block(p * 4 + 2), pl.ds(HALF, HALF)]
        two = self.links.start(right, right, self.a2l[p], "seq", self.flow.al)
        self.second[p] = (one, two)

    def far_a(self, p):
        self.second[p][0].wait_recv()
        self.second[p][1].wait_recv()

    def other_z(self):
        self.zc.wait_recv()
        self.send_a(1)

    def pick(self, order):
        flow, links = self.flow, self.links
        block = self.block(order)
        ids = self.table[block]
        hot = jnp.zeros((LEN, LEN), jnp.float32)
        for k in range(TOP):
            hot = hot + jnp.where(ids[k : k + 1, :] == self.codes, 1.0, 0.0)
        picked = jnp.dot(
            hot.astype(jnp.bfloat16), self.tokens[block], preferred_element_type=jnp.float32
        )
        self.out_buf[:, :, block] = picked.astype(jnp.bfloat16).reshape(4, 2, CAP, WIDTH // 2)
        source = flow.at(z=self.zs[order // 4], da=SHIFTS[order % 4])
        place = self.got.at[:, source, :, flow.cols]
        right = order % 2 == 0
        self.sent[order] = (
            links.start(
                self.out_buf.at[flow.row(2), :, block],
                self.far_buf.at[order],
                self.f1_id[order],
                "seq",
                flow.br if right else flow.bl,
            ),
            links.start(
                self.out_buf.at[flow.row(1), :, block], place, self.r_id[order], "seq", flow.br
            ),
            links.start(
                self.out_buf.at[flow.row(3), :, block], place, self.l_id[order], "seq", flow.bl
            ),
        )
        self.kept.append(
            links.local(self.out_buf.at[flow.b, :, block], place, self.own_id[order])
        )

    def forward_b(self, order):
        flow = self.flow
        right = order % 2 == 0
        self.sent[order][0].wait_recv()
        source = flow.at(
            z=self.zs[order // 4], da=SHIFTS[order % 4], db=3 if right else 1
        )
        self.far[order] = self.links.start(
            self.far_buf.at[order],
            self.got.at[:, source, :, flow.cols],
            self.f2_id[order],
            "seq",
            flow.br if right else flow.bl,
        )

    def finish(self):
        for order in range(8):
            self.sent[order][1].wait_recv()
            self.sent[order][2].wait_recv()
            self.far[order].wait_recv()
        for copy in self.kept:
            copy.wait()


def run_streams(streams):
    def do(name, *given):
        for stream in streams:
            getattr(stream, name)(*given)

    do("pick", 0)
    do("forward_a", 0)
    do("pick", 1)
    do("pick", 2)
    do("other_z")
    do("forward_b", 0)
    do("pick", 4)
    do("far_a", 0)
    do("pick", 3)
    do("forward_b", 1)
    do("forward_b", 2)
    do("forward_a", 1)
    do("pick", 5)
    do("pick", 6)
    do("forward_b", 4)
    do("forward_b", 3)
    do("far_a", 1)
    do("pick", 7)
    for order in (5, 6, 7):
        do("forward_b", order)
    do("finish")


def tell(links, flow, ids, value, out):
    copies = [
        links.start(value, out.at[flow.home], ids[i], "seq", peer)
        for i, peer in enumerate(flow.family())
    ]
    out[flow.home] = value[...]
    return copies


def first_kernel(
    rows, slots, kv_in, got, tokens, table, kv_out, out_buf, far_buf, send, recv
):
    flows = [Flow(0, WIDTH // 2), Flow(1, WIDTH // 2)]
    kv_flows = [Flow(0, HEAD_DIM), Flow(1, HEAD_DIM)]
    links = Links(send, recv)
    greet("seq", all_peers(*flows))
    gathers = [GatherStream(links, flow, kv_in, kv_out) for flow in kv_flows]
    streams = [
        DispatchStream(links, flow, rows, tokens, table, out_buf, far_buf, got) for flow in flows
    ]
    told = []
    for flow in flows:
        told += tell(links, flow, links.ids(7), slots, table.at[flow.which])
    for stream in gathers + streams:
        stream.begin()
    for copy in told:
        copy.wait_recv()
    run_streams(gathers + streams)
    links.finish()


FIRST_SEMS = 2 * 34 + 2 * 49 + 14


def dispatch_first(rows, slots, kv):
    return pl.pallas_call(
        first_kernel,
        name="dispatch_grads",
        out_shape=(
            jax.ShapeDtypeStruct((2, 32, CAP, WIDTH), jnp.bfloat16),
            jax.ShapeDtypeStruct((2, 8, LEN, WIDTH // 2), jnp.bfloat16),
            jax.ShapeDtypeStruct((2, 8, 8, LEN), jnp.int32),
            jax.ShapeDtypeStruct((32, LEN, 2 * HEAD_DIM), jnp.bfloat16),
        ),
        in_specs=[VMEM, VMEM, VMEM],
        out_specs=(ANY, VMEM, VMEM, ANY),
        scratch_shapes=[
            pltpu.VMEM((2, 4, 2, 8, CAP, WIDTH // 2), jnp.bfloat16),
            pltpu.VMEM((2, 8, 2, CAP, WIDTH // 2), jnp.bfloat16),
            pltpu.SemaphoreType.DMA((FIRST_SEMS,)),
            pltpu.SemaphoreType.DMA((FIRST_SEMS,)),
        ],
        compiler_params=params(1),
    )(rows, slots, kv)


def next_kernel(rows, table, got, tokens, out_buf, far_buf, send, recv):
    flows = [Flow(0, WIDTH // 2), Flow(1, WIDTH // 2)]
    links = Links(send, recv)
    greet("seq", near_peers(flows[0]))
    streams = [
        DispatchStream(links, flow, rows, tokens, table, out_buf, far_buf, got) for flow in flows
    ]
    for stream in streams:
        stream.begin()
    run_streams(streams)
    links.finish()


def dispatch_next(rows, table):
    return pl.pallas_call(
        next_kernel,
        name="dispatch_rows",
        out_shape=jax.ShapeDtypeStruct((2, 32, CAP, WIDTH), jnp.bfloat16),
        in_specs=[VMEM, VMEM],
        out_specs=ANY,
        scratch_shapes=[
            pltpu.VMEM((2, 8, LEN, WIDTH // 2), jnp.bfloat16),
            pltpu.VMEM((2, 4, 2, 8, CAP, WIDTH // 2), jnp.bfloat16),
            pltpu.VMEM((2, 8, 2, CAP, WIDTH // 2), jnp.bfloat16),
            pltpu.SemaphoreType.DMA((98,)),
            pltpu.SemaphoreType.DMA((98,)),
        ],
        compiler_params=params(2),
    )(rows, table)


BACK_SHIFTS = [2, 1, 3, 0]


class CollectStream:
    def __init__(self, links, flow, slot, results, scratch, total):
        self.links, self.flow, self.results = links, flow, results
        self.back, self.part, self.far_buf, self.a_half, self.a_full, self.z_buf = (
            ref.at[slot] for ref in scratch
        )
        self.total = total.at[:, flow.cols]
        self.zs = [1 - flow.z, flow.z]
        (self.z_id,) = links.ids(1)
        self.hr, self.hl, self.fr, self.fl = (links.ids(2) for _ in range(4))
        self.r_id, self.l_id, self.f1_id, self.f2_id, self.own_id = (
            links.ids(8) for _ in range(5)
        )
        self.sent, self.far, self.kept, self.halves, self.fulls = {}, {}, {}, {}, {}

    def block(self, order):
        return self.flow.block(self.zs[order // 4], BACK_SHIFTS[order % 4])

    def piece(self, order, db):
        source = self.flow.at(z=self.zs[order // 4], da=BACK_SHIFTS[order % 4], db=db)
        return self.results.at[:, source, :, self.flow.cols]

    def begin(self, order):
        flow, links = self.flow, self.links
        block = self.block(order)
        place = self.back.at[flow.b, :, block]
        right = order % 2 == 0
        self.sent[order] = (
            links.start(
                self.piece(order, 2),
                self.far_buf.at[order],
                self.f1_id[order],
                "seq",
                flow.br if right else flow.bl,
            ),
            links.start(self.piece(order, 1), place, self.r_id[order], "seq", flow.br),
            links.start(self.piece(order, 3), place, self.l_id[order], "seq", flow.bl),
        )
        self.kept[order] = links.local(self.piece(order, 0), place, self.own_id[order])

    def forward_b(self, order):
        flow = self.flow
        right = order % 2 == 0
        self.sent[order][0].wait_recv()
        self.far[order] = self.links.start(
            self.far_buf.at[order],
            self.back.at[flow.row(3 if right else 1), :, self.block(order)],
            self.f2_id[order],
            "seq",
            flow.br if right else flow.bl,
        )

    def arrive(self, order):
        self.kept[order].wait()
        self.sent[order][1].wait_recv()
        self.sent[order][2].wait_recv()
        self.far[order].wait_recv()
        return self.back[:, :, self.block(order)].reshape(LEN, WIDTH // 2)

    def add_on(self, order, summed):
        p, step = order // 4, order % 4
        links, flow = self.links, self.flow
        part = self.part.at[self.block(order)]
        low, high = pl.ds(0, HALF), pl.ds(HALF, HALF)
        if step == 0:
            part[...] = summed.astype(jnp.bfloat16)
            self.halves[p] = (
                links.start(part.at[low], self.a_half.at[p, 0], self.hr[p], "seq", flow.ar),
                links.start(part.at[high], self.a_half.at[p, 1], self.hl[p], "seq", flow.al),
            )
        elif step in (1, 2):
            side = step - 1
            self.halves[p][side].wait_recv()
            arrived = self.a_half[p, side].astype(jnp.float32)
            top, bottom = summed[:HALF], summed[HALF:]
            if side == 0:
                top = top + arrived
            else:
                bottom = bottom + arrived
            part[low] = top.astype(jnp.bfloat16)
            part[high] = bottom.astype(jnp.bfloat16)
            self.fulls[p, side] = links.start(
                part,
                self.a_full.at[p, side],
                (self.fr if side == 0 else self.fl)[p],
                "seq",
                flow.ar if side == 0 else flow.al,
            )
        elif p == 0:
            part[...] = summed.astype(jnp.bfloat16)
        else:
            self.total[...] = summed

    def line_sum(self, p):
        self.fulls[p, 0].wait_recv()
        self.fulls[p, 1].wait_recv()
        return self.a_full[p, 0].astype(jnp.float32) + self.a_full[p, 1].astype(jnp.float32)

    def send_z(self):
        part = self.part.at[self.block(3)]
        part[...] = (part[...].astype(jnp.float32) + self.line_sum(0)).astype(jnp.bfloat16)
        self.zc = self.links.start(part, self.z_buf, self.z_id, "seq", self.flow.zp)

    def finish(self):
        self.total[...] = self.total[...] + self.line_sum(1)
        self.zc.wait_recv()
        self.total[...] = self.total[...] + self.z_buf[...].astype(jnp.float32)


def collect_kernel(
    results, back_results, table, gates, tokens, total, back_total, gate_sum,
    gates_all, back, part, far_buf, a_half, a_full, z_buf, grad_part, grad_got, send, recv,
):
    flows = [Flow(0, WIDTH // 2), Flow(1, WIDTH // 2)]
    links = Links(send, recv)
    greet("seq", all_peers(*flows))
    scratch = (back, part, far_buf, a_half, a_full, z_buf)
    pairs = [
        [
            CollectStream(links, flow, flow.which, results, scratch, total),
            CollectStream(links, flow, 2 + flow.which, back_results, scratch, back_total),
        ]
        for flow in flows
    ]
    streams = [pairs[0][0], pairs[1][0], pairs[0][1], pairs[1][1]]
    told = []
    for flow in flows:
        told += tell(links, flow, links.ids(7), gates, gates_all.at[flow.which])
    for order in range(8):
        for stream in streams:
            stream.begin(order)
    for copy in told:
        copy.wait_recv()
    codes = [flow.codes() for flow in flows]
    g_id = [links.ids(8), links.ids(8)]
    grads_sent = []

    def do(name, *given):
        for stream in streams:
            getattr(stream, name)(*given)

    def combine(order):
        for flow in flows:
            k = flow.which
            forward, backward = pairs[k]
            block = forward.block(order)
            ids, weight = table[k, block], gates_all[k, block]
            mix = jnp.zeros((LEN, LEN), jnp.float32)
            for c in range(TOP):
                mix = mix + jnp.where(ids[c : c + 1, :] == codes[k], weight[c : c + 1, :], 0.0)
            mix = mix.astype(jnp.bfloat16)
            for stream in (forward, backward):
                rows = stream.arrive(order)
                summed = lax.dot_general(
                    mix, rows, (((0,), (0,)), ((), ())), preferred_element_type=jnp.float32
                )
                stream.add_on(order, summed)
                if stream is backward:
                    continue
                dots = lax.dot_general(
                    rows,
                    tokens[k, block],
                    (((1,), (1,)), ((), ())),
                    preferred_element_type=jnp.float32,
                )
                for c in range(TOP):
                    grad_part[k, order, c : c + 1, :] = jnp.sum(
                        jnp.where(ids[c : c + 1, :] == codes[k], dots, 0.0),
                        axis=0,
                        keepdims=True,
                    )
                grad_part[k, order, TOP:, :] = jnp.zeros((8 - TOP, LEN), jnp.float32)
                if order < 7:
                    peer = flow.at(z=forward.zs[order // 4], da=BACK_SHIFTS[order % 4])
                    grads_sent.append(
                        links.start(
                            grad_part.at[k, order],
                            grad_got.at[k, order],
                            g_id[k][order],
                            "seq",
                            peer,
                        )
                    )

    do("forward_b", 0)
    do("forward_b", 1)
    combine(0)
    do("forward_b", 2)
    combine(1)
    do("forward_b", 3)
    combine(2)
    do("forward_b", 4)
    combine(3)
    do("forward_b", 5)
    combine(4)
    do("send_z")
    do("forward_b", 6)
    do("forward_b", 7)
    combine(5)
    combine(6)
    combine(7)
    do("finish")
    gathered = grad_part[0, 7] + grad_part[1, 7]
    for copy in grads_sent:
        copy.wait_recv()
    for k in range(2):
        for order in range(7):
            gathered = gathered + grad_got[k, order]
    gate_sum[...] = gathered
    links.finish()


COLLECT_SEMS = 4 * 49 + 14 + 16


def collect(results, back_results, table, gates, tokens):
    half = WIDTH // 2
    return pl.pallas_call(
        collect_kernel,
        name="collect",
        out_shape=(
            jax.ShapeDtypeStruct((LEN, WIDTH), jnp.float32),
            jax.ShapeDtypeStruct((LEN, WIDTH), jnp.float32),
            jax.ShapeDtypeStruct((8, LEN), jnp.float32),
        ),
        in_specs=[ANY, ANY, VMEM, VMEM, VMEM],
        out_specs=(VMEM, VMEM, VMEM),
        scratch_shapes=[
            pltpu.VMEM((2, 8, 8, LEN), jnp.float32),
            pltpu.VMEM((4, 4, 2, 8, CAP, half), jnp.bfloat16),
            pltpu.VMEM((4, 8, LEN, half), jnp.bfloat16),
            pltpu.VMEM((4, 8, 2, CAP, half), jnp.bfloat16),
            pltpu.VMEM((4, 2, 2, HALF, half), jnp.bfloat16),
            pltpu.VMEM((4, 2, 2, LEN, half), jnp.bfloat16),
            pltpu.VMEM((4, LEN, half), jnp.bfloat16),
            pltpu.VMEM((2, 8, 8, LEN), jnp.float32),
            pltpu.VMEM((2, 7, 8, LEN), jnp.float32),
            pltpu.SemaphoreType.DMA((COLLECT_SEMS,)),
            pltpu.SemaphoreType.DMA((COLLECT_SEMS,)),
        ],
        compiler_params=params(3),
    )(results, back_results, table, gates, tokens)


def small_sum_kernel(part, total, got, send, recv):
    me = lax.axis_index("grp")
    links = Links(send, recv)
    peers = [(me + shift) % 8 for shift in range(1, 8)]
    ids = links.ids(7)
    greet("grp", peers)
    copies = [
        links.start(part, got.at[me], ids[i], "grp", peers[i]) for i in range(7)
    ]
    got[me] = part[...]
    for copy in copies:
        copy.wait_recv()
    summed = got[0]
    for i in range(1, 8):
        summed = summed + got[i]
    total[...] = summed
    links.finish()


def small_sum(part, collective_id, name):
    shape = part.shape
    return pl.pallas_call(
        small_sum_kernel,
        name=name,
        out_shape=jax.ShapeDtypeStruct(shape, jnp.float32),
        in_specs=[VMEM],
        out_specs=VMEM,
        scratch_shapes=[
            pltpu.VMEM((8,) + shape, jnp.float32),
            pltpu.SemaphoreType.DMA((7,)),
            pltpu.SemaphoreType.DMA((7,)),
        ],
        compiler_params=params(collective_id),
    )(part)


CHUNK = 32
CHUNKS = 256 // CHUNK


def hidden_kernel(part, total, held, sibling, arrived, send, recv):
    me = lax.axis_index("grp")
    core, chip = me % 2, me // 2
    high = chip // 2
    depth = chip + high * (3 - 2 * chip)
    twin = chip * 2 + 1 - core
    inner = me + 2 - 4 * high
    outer = (me + 6 + 4 * high) % 8
    links = Links(send, recv)
    pair_id, chain_id, spread_id, share_id = (links.ids(2 * CHUNKS) for _ in range(4))
    outgoing, incoming = 1 - high, high
    barrier = pltpu.get_barrier_semaphore()
    for peer in (twin, inner):
        pl.semaphore_signal(barrier, inc=1, device_id={"grp": peer}, device_id_type=MESH)

    @pl.when(depth == 1)
    def _():
        pl.semaphore_signal(barrier, inc=1, device_id={"grp": outer}, device_id_type=MESH)
        pl.semaphore_wait(barrier, 3)

    @pl.when(depth == 0)
    def _():
        pl.semaphore_wait(barrier, 2)

    def local(stream, i):
        return pl.ds(pl.multiple_of(stream * 256 + i * CHUNK, CHUNK), CHUNK)

    def whole(half, stream, i):
        return pl.ds(pl.multiple_of(half * 512 + stream * 256 + i * CHUNK, CHUNK), CHUNK)

    def pair(stream, i):
        return links.copy(
            part.at[whole(1 - core, stream, i)],
            sibling.at[local(stream, i)],
            pair_id[0] + stream * CHUNKS + i,
            "grp",
            twin,
        )

    def chain(stream, i, peer):
        spot = local(stream, i)
        return links.copy(
            held.at[spot], arrived.at[spot], chain_id[0] + stream * CHUNKS + i, "grp", peer
        )

    def spread(stream, i, peer):
        spot = total.at[whole(core, stream, i)]
        return links.copy(spot, spot, spread_id[0] + stream * CHUNKS + i, "grp", peer)

    def share(stream, i):
        spot = total.at[whole(core, stream, i)]
        return links.copy(spot, spot, share_id[0] + stream * CHUNKS + i, "grp", twin)

    for i in range(CHUNKS):
        pair(outgoing, i).start()
        pair(incoming, i).start()

    def own_sum(stream, i):
        pair(stream, i).wait_recv()
        return part[whole(core, stream, i)].astype(jnp.float32) + sibling[
            local(stream, i)
        ].astype(jnp.float32)

    @pl.when(depth == 0)
    def _():
        for i in range(CHUNKS):
            held[local(outgoing, i)] = own_sum(outgoing, i).astype(jnp.bfloat16)
            chain(outgoing, i, inner).start()
        for i in range(CHUNKS):
            own = own_sum(incoming, i)
            chain(incoming, i, inner).wait_recv()
            total[whole(core, incoming, i)] = (
                own + arrived[local(incoming, i)].astype(jnp.float32)
            ).astype(jnp.bfloat16)
            spread(incoming, i, inner).start()
            share(incoming, i).start()
        for i in range(CHUNKS):
            spread(outgoing, i, inner).wait_recv()
            share(outgoing, i).start()
        for i in range(CHUNKS):
            chain(outgoing, i, inner).wait_send()
            spread(incoming, i, inner).wait_send()

    @pl.when(depth == 1)
    def _():
        def pass_on(stream, i, source, target):
            own = own_sum(stream, i)
            chain(stream, i, source).wait_recv()
            held[local(stream, i)] = (
                own + arrived[local(stream, i)].astype(jnp.float32)
            ).astype(jnp.bfloat16)
            chain(stream, i, target).start()

        def hand_out(stream, i, source, target):
            spread(stream, i, source).wait_recv()
            spread(stream, i, target).start()
            share(stream, i).start()

        for i in range(CHUNKS):
            pass_on(outgoing, i, outer, inner)
            pass_on(incoming, i, inner, outer)
        for i in range(CHUNKS):
            hand_out(incoming, i, outer, inner)
            hand_out(outgoing, i, inner, outer)
        for i in range(CHUNKS):
            chain(outgoing, i, inner).wait_send()
            chain(incoming, i, outer).wait_send()
            spread(incoming, i, inner).wait_send()
            spread(outgoing, i, outer).wait_send()

    for i in range(CHUNKS):
        for stream in (0, 1):
            pair(stream, i).wait_send()
            share(stream, i).wait()


def hidden_sum(part):
    sems = 8 * CHUNKS
    return pl.pallas_call(
        hidden_kernel,
        name="hidden_sum",
        out_shape=jax.ShapeDtypeStruct((1024, FF), jnp.bfloat16),
        in_specs=[VMEM],
        out_specs=VMEM,
        scratch_shapes=[
            pltpu.VMEM((512, FF), jnp.bfloat16),
            pltpu.VMEM((512, FF), jnp.bfloat16),
            pltpu.VMEM((512, FF), jnp.bfloat16),
            pltpu.SemaphoreType.DMA((sems,)),
            pltpu.SemaphoreType.DMA((sems,)),
        ],
        compiler_params=params(5),
    )(part)


KEYS = 512


def attend_kernel(bounds, query, kv, first_key, query_pos, inputs, resid, best, total, acc):
    scale = HEAD_DIM ** (-0.5) * 1.4426950408889634
    groups = HEADS // KV_HEADS
    best[...] = jnp.full(best.shape, -1e30, jnp.float32)
    total[...] = jnp.zeros(total.shape, jnp.float32)
    acc[...] = jnp.zeros(acc.shape, jnp.float32)

    def step(masked, i, carry):
        start = pl.multiple_of(i * KEYS, KEYS)
        keys = kv[pl.ds(start, KEYS), pl.ds(0, HEAD_DIM)]
        values = kv[pl.ds(start, KEYS), pl.ds(HEAD_DIM, HEAD_DIM)]
        if masked:
            key_pos = start + lax.broadcasted_iota(jnp.int32, (LEN, KEYS), 1)
            allowed = (key_pos <= query_pos[...]) & (key_pos >= first_key[...])
        for h in range(groups):
            scores = lax.dot_general(
                query[:, h * HEAD_DIM : (h + 1) * HEAD_DIM],
                keys,
                (((1,), (1,)), ((), ())),
                preferred_element_type=jnp.float32,
            )
            if masked:
                scores = jnp.where(allowed, scores, -1e30)
            old = best[h]
            new = jnp.maximum(old, jnp.max(scores, axis=1, keepdims=True))
            weights = jnp.exp2((scores - new) * scale)
            shrink = jnp.exp2((old - new) * scale)
            best[h] = new
            total[h] = total[h] * shrink + jnp.sum(weights, axis=1, keepdims=True)
            acc[h] = acc[h] * shrink + jnp.dot(
                weights.astype(jnp.bfloat16), values, preferred_element_type=jnp.float32
            )
        return carry

    lax.fori_loop(bounds[0], bounds[1], functools.partial(step, True), 0)
    lax.fori_loop(bounds[1], bounds[2], functools.partial(step, False), 0)
    lax.fori_loop(bounds[2], bounds[3], functools.partial(step, True), 0)
    for h in range(groups):
        cols = slice(h * HEAD_DIM, (h + 1) * HEAD_DIM)
        attended = (acc[h] / total[h]).astype(jnp.bfloat16).astype(jnp.float32)
        resid[:, cols] = (inputs[:, cols].astype(jnp.float32) + attended).astype(jnp.bfloat16)


def attend(query, kv, doc_ids, inputs):
    first_query = lax.axis_index("seq") * LEN
    query_pos = first_query + jnp.arange(LEN, dtype=jnp.int32)
    query_doc = lax.dynamic_slice_in_dim(doc_ids, first_query, LEN)
    first_key = jnp.sum(
        (doc_ids[None, :] < query_doc[:, None]).astype(jnp.int32), axis=1, keepdims=True
    )
    low = first_key[0, 0] // KEYS
    high = (first_query + LEN + KEYS - 1) // KEYS
    full_low = jnp.minimum((first_key[LEN - 1, 0] + KEYS - 1) // KEYS, high)
    full_high = jnp.maximum((first_query + 1) // KEYS, full_low)
    bounds = jnp.stack([low, full_low, full_high, high])
    groups = HEADS // KV_HEADS
    return pl.pallas_call(
        attend_kernel,
        name="attend",
        out_shape=jax.ShapeDtypeStruct((LEN, WIDTH), jnp.bfloat16),
        in_specs=[pl.BlockSpec(memory_space=pltpu.SMEM)] + [VMEM] * 5,
        out_specs=VMEM,
        scratch_shapes=[
            pltpu.VMEM((groups, LEN, 1), jnp.float32),
            pltpu.VMEM((groups, LEN, 1), jnp.float32),
            pltpu.VMEM((groups, LEN, HEAD_DIM), jnp.float32),
        ],
        compiler_params=params(),
    )(bounds.astype(jnp.int32), query, kv, first_key, query_pos[:, None], inputs)


def product_kernel(turned, rows, weight, out):
    out[0] = lax.dot_general(
        rows[0],
        weight[0],
        (((1,), (1 if turned else 0,)), ((), ())),
        preferred_element_type=jnp.float32,
    ).astype(jnp.bfloat16)


def product(rows, weight, turned, name):
    sets, count, depth = rows.shape
    width = weight.shape[1 if turned else 2]
    return pl.pallas_call(
        functools.partial(product_kernel, turned),
        name=name,
        grid=(sets,),
        out_shape=jax.ShapeDtypeStruct((sets, count, width), jnp.bfloat16),
        in_specs=[
            pl.BlockSpec((1, count, depth), lambda m: (m, 0, 0)),
            pl.BlockSpec((1,) + weight.shape[1:], lambda m: (m, 0, 0)),
        ],
        out_specs=pl.BlockSpec((1, count, width), lambda m: (m, 0, 0)),
        compiler_params=params(),
        cost_estimate=pl.CostEstimate(
            flops=2 * sets * count * depth * width,
            bytes_accessed=2 * sets * (count * depth + depth * width + count * width),
            transcendentals=0,
        ),
    )(rows, weight)


def expert_kernel(pre, act_grad, w_out, w_in, out, grad):
    root = 0.7978845608028654
    wide = pre[0].astype(jnp.float32)
    square = wide * wide
    curve = jnp.tanh(root * wide * (1.0 + 0.044715 * square))
    active = (0.5 * wide * (1.0 + curve)).astype(jnp.bfloat16)
    out[0] = jnp.dot(active, w_out[0], preferred_element_type=jnp.float32).astype(jnp.bfloat16)
    slope = 0.5 * (1.0 + curve) + (0.5 * root) * wide * (1.0 - curve * curve) * (
        1.0 + 3 * 0.044715 * square
    )
    pre_grad = (slope * act_grad[0].astype(jnp.float32)).astype(jnp.bfloat16)
    grad[0] = lax.dot_general(
        pre_grad, w_in[0], (((1,), (1,)), ((), ())), preferred_element_type=jnp.float32
    ).astype(jnp.bfloat16)


def expert_products(pre, act_grad, w_out, w_in):
    sets, count, _ = pre.shape
    tile = 256

    def moving(width):
        return pl.BlockSpec((1, tile, width), lambda m, i: (m, i, 0))

    def held(weight):
        return pl.BlockSpec((1,) + weight.shape[1:], lambda m, i: (m, 0, 0))

    shape = jax.ShapeDtypeStruct((sets, count, WIDTH), jnp.bfloat16)
    return pl.pallas_call(
        expert_kernel,
        name="expert_products",
        grid=(sets, count // tile),
        out_shape=(shape, shape),
        in_specs=[moving(FF), moving(FF), held(w_out), held(w_in)],
        out_specs=(moving(WIDTH), moving(WIDTH)),
        compiler_params=params(),
        cost_estimate=pl.CostEstimate(
            flops=4 * sets * count * FF * WIDTH,
            bytes_accessed=4 * sets * (count * (FF + WIDTH) + FF * WIDTH),
            transcendentals=sets * count * FF,
        ),
    )(pre, act_grad, w_out, w_in)


def body(
    inputs,
    query_states,
    key_states,
    value_states,
    doc_ids,
    modality,
    expert_ids,
    norm_gain,
    router_w,
    w_in,
    w_out,
    grad_out,
):
    length, width = inputs.shape
    experts = lax.axis_size("seq")
    kept_mask = expert_ids >= 0
    kept_wide = kept_mask.astype(jnp.float32)
    column = modality[:, None] * experts + jnp.where(kept_mask, expert_ids, 0)
    one_hot = (
        column[:, :, None] == jnp.arange(2 * experts, dtype=jnp.int32)[None, None, :]
    ) & kept_mask[:, :, None]
    entries = length * TOP
    flat_hot = one_hot.reshape(entries, 2 * experts).astype(jnp.bfloat16)
    entry_range = jnp.arange(entries, dtype=jnp.int32)
    earlier = (entry_range[:, None] > entry_range[None, :]).astype(jnp.bfloat16)
    before = jnp.dot(earlier, flat_hot, preferred_element_type=jnp.float32)
    slot_rank = jnp.sum(before * flat_hot.astype(jnp.float32), axis=1).astype(jnp.int32)
    slots = jnp.where(kept_mask, column * CAP + slot_rank.reshape(length, TOP), -1)
    slots = jnp.concatenate([slots.T, jnp.full((8 - TOP, length), -1, jnp.int32)], axis=0)

    w_in_local = w_in[:, 0]
    w_out_local = w_out[:, 0]

    got_grads, tokens_grad, table, kv = dispatch_first(
        grad_out, slots, jnp.concatenate([key_states, value_states], axis=1)
    )
    partial_back = product(
        got_grads.reshape(2, experts * CAP, width), w_out_local, True, "back_product"
    )
    act_grad = lax.psum(partial_back, "grp")

    resid_state = attend(query_states, kv.reshape(experts * length, 2 * HEAD_DIM), doc_ids, inputs)
    state_wide = resid_state.astype(jnp.float32)
    scaled = state_wide * norm_gain[None, :]
    raw_part = lax.dot_general(
        router_w,
        scaled.astype(jnp.bfloat16),
        (((0,), (1,)), ((), ())),
        preferred_element_type=jnp.float32,
    )
    square_part = jnp.sum(state_wide * state_wide, axis=1)[None, :]
    stats = small_sum(
        jnp.concatenate([raw_part, square_part, jnp.zeros((7, length), jnp.float32)], axis=0),
        6,
        "sum_stats",
    )
    inv_row = lax.rsqrt(stats[2 * experts] / D + eps_norm)
    inv_rms = inv_row[:, None]
    raw_logits = stats[: 2 * experts].T
    logits = raw_logits * inv_rms
    normed = (scaled * inv_rms).astype(jnp.bfloat16)
    chosen = jnp.sum(jnp.where(one_hot, logits[:, None, :], 0.0), axis=2)
    lifted = jax.nn.sigmoid(chosen)
    denominator = gate_offset + jnp.sum(kept_wide * lifted, axis=1, keepdims=True)
    gates = kept_wide * lifted / denominator
    gates_t = jnp.concatenate([gates.T, jnp.zeros((8 - TOP, length), jnp.float32)], axis=0)

    got_rows = dispatch_next(normed, table)
    partial_value = product(
        got_rows.reshape(2, experts * CAP, width), w_in_local, False, "row_product"
    )
    pre_act = hidden_sum(partial_value.reshape(2 * experts * CAP, FF)).reshape(
        2, experts * CAP, FF
    )
    expert_out, entry_grad = expert_products(pre_act, act_grad, w_out_local, w_in_local)
    mixture, entry_sum, gate_part = collect(
        expert_out.reshape(2, experts, CAP, width),
        entry_grad.reshape(2, experts, CAP, width),
        table,
        gates_t,
        tokens_grad,
    )
    layer_out = (state_wide + mixture).astype(jnp.bfloat16)
    entry_dot = jnp.sum(entry_sum * scaled, axis=1)[None, :]
    row_index = jnp.arange(8, dtype=jnp.int32)[:, None]
    ends = small_sum(jnp.where(row_index == TOP, entry_dot, gate_part), 7, "sum_ends")
    gate_grad = ends[:TOP].T
    gate_dot = jnp.sum(gates * gate_grad, axis=1, keepdims=True)
    logit_grad = kept_wide * (gate_grad - gate_dot) / denominator * lifted * (1.0 - lifted)
    logit_full = jnp.sum(jnp.where(one_hot, logit_grad[:, :, None], 0.0), axis=1)
    router_grad = jnp.dot(
        logit_full, router_w.astype(jnp.float32).T, precision=lax.Precision.HIGHEST
    )
    norm_dot = ends[TOP][:, None] + jnp.sum(logit_full * raw_logits, axis=1, keepdims=True)
    normed_grad = router_grad + entry_sum
    state_grad = (
        grad_out.astype(jnp.float32)
        + inv_rms * norm_gain[None, :] * normed_grad
        - inv_rms**3 / D * state_wide * norm_dot
    )
    return (layer_out, state_grad.astype(jnp.bfloat16))


def solution(mesh):
    in_specs = (
        P("seq", "grp"),
        P("seq", "grp"),
        P("seq", "grp"),
        P("seq", "grp"),
        P(),
        P("seq"),
        P("seq", None),
        P("grp"),
        P("grp", None),
        P(None, "seq", "grp", None),
        P(None, "seq", None, "grp"),
        P("seq", "grp"),
    )
    out_specs = (P("seq", "grp"), P("seq", "grp"))
    return jax.shard_map(body, mesh=mesh, in_specs=in_specs, out_specs=out_specs, check_vma=False)
```

time: 652 us -> 353 us (0.54)
  waiting for transfers between devices: 413 us -> 0.02 us
  Pallas kernels: 0 us -> 312 us
  blocking collectives: 104 us -> 0 us
  matrix products: 48.5 us -> 3.76 us
  starting transfers between devices: 33.5 us -> 0.04 us
  local copies, waits for them, and re-layouts: 20.5 us -> 4.06 us
    pallas_call x0 -> x10, Pallas kernels: none -> 312 us  [the longest x1 79.4 us: hidden_sum(): pl.pallas_call(hidden_kernel, name='hidden_sum', out_shape=jax.ShapeDtype...]
    all_gather x2 -> x0, waiting for transfers between devices: 148 us -> none  [the longest x1 79.9 us: attend(): key_piece = lax.all_gather(key_states, 'seq', axis=0, tiled=True)]
    psum x1, waiting for transfers between devices: 136 us -> 0.01 us  [body(): act_grad = lax.psum(partial_back, 'grp')]
    all_to_all x4 -> x0, waiting for transfers between devices: 128 us -> none  [the longest x2 88.4 us: dispatch(): lax.all_to_all(buffers, 'seq', split_axis=1, concat_axis=1, tiled=True)]
    psum x4 -> x0, blocking collectives: 104 us -> none  [row_total(): return lax.psum(partial_value, 'grp')]
    dot_general x12 -> x1, matrix products: 47.6 us -> 1.16 us  [body(): lax.dot_general(router_w, scaled.astype(jnp.bfloat16), (((0,), (1,)), (()...]
    all_to_all x4 -> x0, starting transfers between devices: 33.4 us -> none  [the longest x2 18.6 us: collect(): lax.all_to_all(buffers, 'seq', split_axis=1, concat_axis=1, tiled=True)]
    convert_element_type x3 -> x1, other arithmetic: 9.76 us -> 1.76 us  [body(): normed = (scaled * inv_rms).astype(jnp.bfloat16)]
  transfers between devices with their start and end apart: 7 -> 1, of which waited for: 6 -> 0; matrix products, arithmetic and copies ran while one was open for 6% -> 3% of each run, Pallas kernels for 0% -> 47%
where the time goes in v2:
time: 353 us; the launch traced here: 352 us
  Pallas kernels  312 us (88%)
  between operations  17.5 us (5%)
  other arithmetic  14.3 us (4%)
  local copies, waits for them, and re-layouts  4.06 us (1%)
  matrix products  3.76 us (1%)
    pallas_call x1, Pallas kernels, hidden_sum(): pl.pallas_call(hidden_kernel, name='hidden_sum', out_shape=jax.ShapeDtype...  79.4 us
    pallas_call x1, Pallas kernels, collect(): pl.pallas_call(collect_kernel, name='collect', out_shape=(jax.ShapeDtypeS...  69.6 us
    pallas_call x1, Pallas kernels, dispatch_next(): pl.pallas_call(next_kernel, name='dispatch_rows', out_shape=jax.ShapeDtyp...  52.8 us
    pallas_call x1, Pallas kernels, dispatch_first(): pl.pallas_call(first_kernel, name='dispatch_grads', out_shape=(jax.ShapeD...  49.9 us
    pallas_call x2, Pallas kernels, small_sum(): pl.pallas_call(small_sum_kernel, name=name, out_shape=jax.ShapeDtypeStruc...  26.9 us
    pallas_call x1, Pallas kernels, expert_products(): pl.pallas_call(expert_kernel, name='expert_products', grid=(sets, count /...  14 us
    pallas_call x2, Pallas kernels, product(): pl.pallas_call(functools.partial(product_kernel, turned), name=name, grid...  13.9 us
  transfers between devices with their start and end apart: 1, of which 0 were waited for; matrix products, arithmetic and copies ran while one was open for 3% of the time, Pallas kernels for 47%

profile of v2, /device:TPU:1, one launch (start us, length us, event | category | flops | bytes accessed | tf_op | source)
XLA Modules:
  0.0 351.8 jit_solution(6691331667436357565)
XLA Ops:
  7.2 0.0 copy-start
  7.2 0.0 all-reduce.4.cloned.1.call-start
  7.2 0.7 broadcast_multiply_fusion
  7.9 0.7 select_add_fusion
  8.6 0.1 copy.27
  8.7 0.1 eq.30
  8.8 0.1 copy.28
  9.0 0.1 and.37
  9.1 0.3 fusion.4
  9.4 0.1 convert_element_type.41
  9.5 0.1 copy.29
  9.6 0.6 concatenate.12.slots
  10.2 1.4 pad_maximum_fusion.kv_in
  11.6 49.9 %dispatch_grads.1 = (bf16[2,32,16,1024]{3,2,1,0:T(8,128)(2,1)}, bf16[2,8,128,512]{3,2,1,0:T(8,128)(2,1)}, s32[2,8,8,128]{3,2,1,0:T(8,128)}, bf16[32,128,256]{2,1,0:T(8,128)(2,1)}) custom-call(bf16[128,1024]{1,0:T(8,128)(2,1)} %rows.1, s32[8,128]{1,0:T(8,128)} %concatenate.12.slots, bf16[128,256]{1,0:T(8,128)(2,1)} %pad_maximum_fusion.kv_in), custom_call_target="tpu_custom_call" | custom-call | tf_op jit(solution)/shard_map/dispatch_grads/pallas_call | solution.py:370
  61.5 7.0 %back_product.1 = bf16[2,512,1408]{2,1,0:T(8,128)(2,1)} custom-call(bf16[2,512,1024]{2,1,0:T(8,128)(2,1)} %bitcast.57, bf16[2,1408,1024]{2,1,0:T(8,128)(2,1)} %bitcast.55), custom_call_target="tpu_custom_call" | custom-call | flops 2952790016 | bytes 10747904 | tf_op jit(solution)/shard_map/back_product/pallas_call | solution.py:930
  68.5 0.0 copy-start.5
  68.5 0.0 all-reduce.4.cloned.1.call-update
  68.5 0.0 copy-start.4
  68.5 0.7 copy-done.5
  69.2 0.1 dynamic_slice.3
  69.3 0.4 convert_reduce_fusion
  69.6 0.6 fusion.28
  73.5 0.7 copy.30.first_key
  74.2 0.1 pad.4.clone
  74.3 0.7 pad_add_fusion.bounds
  75.0 0.6 iota_add_fusion.query_pos
  75.6 5.8 %attend.1 = bf16[128,1024]{1,0:T(8,128)(2,1)} custom-call(s32[4]{0:T(128)} %pad_add_fusion.bounds, bf16[128,1024]{1,0:T(8,128)(2,1)} %query.1, bf16[4096,256]{1,0:T(8,128)(2,1)} %bitcast.47, s32[128,1]{1,0:T(8,128)} %copy.30.first_key, s32[128,1]{1,0:T(8,128)} %iota_add_fusion.query_pos, bf16[128,1024]{1,0:T(8,128)(2,1)} %inputs.1), custom_call_target="tpu_custom_call" | custom-call | tf_op jit(solution)/shard_map/attend/pallas_call | solution.py:903
  81.4 1.1 fusion.10
  82.4 0.0 copy-done
  82.4 0.0 copy-done.4
  82.5 1.2 convolution_bitcast_fusion
  83.6 0.7 maximum_maximum_fusion.part
  84.3 19.1 %sum_stats.1 = f32[72,128]{1,0:T(8,128)} custom-call(f32[72,128]{1,0:T(8,128)} %maximum_maximum_fusion.part), custom_call_target="tpu_custom_call" | custom-call | tf_op jit(solution)/shard_map/sum_stats/pallas_call | solution.py:690
  103.4 0.7 fusion.26
  104.1 1.8 fusion.8.rows
  105.9 52.8 %dispatch_rows.1 = bf16[2,32,16,1024]{3,2,1,0:T(8,128)(2,1)} custom-call(bf16[128,1024]{1,0:T(8,128)(2,1)} %fusion.8.rows, s32[2,8,8,128]{3,2,1,0:T(8,128)} %get-tuple-element.12.table), custom_call_target="tpu_custom_call" | custom-call | tf_op jit(solution)/shard_map/dispatch_rows/pallas_call | solution.py:405
  158.6 6.9 %row_product.1 = bf16[2,512,1408]{2,1,0:T(8,128)(2,1)} custom-call(bf16[2,512,1024]{2,1,0:T(8,128)(2,1)} %bitcast.48, bf16[2,1024,1408]{2,1,0:T(8,128)(2,1)} %bitcast.53), custom_call_target="tpu_custom_call" | custom-call | flops 2952790016 | bytes 10747904 | tf_op jit(solution)/shard_map/row_product/pallas_call | solution.py:930
  165.5 0.0 copy-start.3
  165.5 79.4 %hidden_sum.1 = bf16[1024,1408]{1,0:T(8,128)(2,1)} custom-call(bf16[1024,1408]{1,0:T(8,128)(2,1)} %bitcast.46), custom_call_target="tpu_custom_call" | custom-call | tf_op jit(solution)/shard_map/hidden_sum/pallas_call | solution.py:827
  244.9 0.0 copy-done.3
  245.0 0.6 concatenate.15.gates
  245.7 0.0 all-reduce.4.cloned.1.call-done.act_grad
  245.7 14.0 %expert_products.1 = (bf16[2,512,1024]{2,1,0:T(8,128)(2,1)}, bf16[2,512,1024]{2,1,0:T(8,128)(2,1)}) custom-call(bf16[2,512,1408]{2,1,0:T(8,128)(2,1)} %bitcast.45, bf16[2,512,1408]{2,1,0:T(8,128)(2,1)} %all-reduce.4.cloned.1.call-done.act_grad, bf16[2,1408,1024]{2,1,0:T(8,128)(2,1)} %bitcast.56, bf16[2,1024,1408]{2,1,0:T(8,128)(2,1)} %bitcast.54), custom_call_target="tpu_custom_call" | custom-call | flops 5905580032 | bytes 21495808 | tf_op jit(solution)/shard_map/expert_products/pallas_call | solution.py:976
  259.7 0.0 copy-start.1
  259.7 0.0 copy-start.2
  259.7 69.6 %collect.1 = (f32[128,1024]{1,0:T(8,128)}, f32[128,1024]{1,0:T(8,128)}, f32[8,128]{1,0:T(8,128)}) custom-call(bf16[2,32,16,1024]{3,2,1,0:T(8,128)(2,1)} %bitcast.49, bf16[2,32,16,1024]{3,2,1,0:T(8,128)(2,1)} %bitcast.50, s32[2,8,8,128]{3,2,1,0:T(8,128)} %get-tuple-element.12.table, f32[8,128]{1,0:T(8,128)} %concatenate.15.gates, ...), custom_call_target="tpu_custom_call" | custom-call | tf_op jit(solution)/shard_map/collect/pallas_call | solution.py:642
  329.3 0.0 copy-done.1
  329.4 2.0 fusion.9
  331.4 1.3 broadcast_select_fusion.part
  332.7 7.8 %sum_ends.1 = f32[8,128]{1,0:T(8,128)} custom-call(f32[8,128]{1,0:T(8,128)} %broadcast_select_fusion.part), custom_call_target="tpu_custom_call" | custom-call | tf_op jit(solution)/shard_map/sum_ends/pallas_call | solution.py:690
  340.5 0.7 fusion.23
  341.2 0.7 fusion.22
  342.0 0.7 bitcast_add_fusion
  342.7 0.0 copy-done.2
  342.7 2.3 fusion.3
  (11 shorter events, 0.2 us)
Async XLA Ops:
  7.2 75.3 %copy-start = (bf16[1024,64]{0,1:T(8,128)(2,1)S(1)}, bf16[1024,64]{0,1:T(8,128)(2,1)}, u32[]{:S(2)}) copy-start(bf16[1024,64]{0,1:T(8,128)(2,1)} %param.20) | copy-start | bytes 393220
  7.2 238.5 %all-reduce.4.cloned.1.call-start = ((), (), s32[]{:S(2)}) async-start(), calls=%async_computation | async-start | bytes 5767168 | tf_op jit(solution)/shard_map/psum | solution.py:1032
  68.5 0.7 copy-start.5
  68.5 13.9 %copy-start.4 = (f32[1024]{0:T(1024)S(1)}, f32[1024]{0:T(1024)}, u32[]{:S(2)}) copy-start(f32[1024]{0:T(1024)} %param.19) | copy-start | bytes 12292
  165.5 79.4 %copy-start.3 = (f32[72,128]{1,0:T(8,128)S(1)}, f32[72,128]{1,0:T(8,128)}, u32[]{:S(2)}) copy-start(f32[72,128]{1,0:T(8,128)} %sum_stats.1) | copy-start | bytes 110596
  259.7 69.6 %copy-start.1 = (bf16[128,1024]{1,0:T(8,128)(2,1)S(1)}, bf16[128,1024]{1,0:T(8,128)(2,1)}, u32[]{:S(2)}) copy-start(bf16[128,1024]{1,0:T(8,128)(2,1)} %attend.1) | copy-start | bytes 786436
  259.7 82.9 %copy-start.2 = (bf16[128,1024]{1,0:T(8,128)(2,1)S(1)}, bf16[128,1024]{1,0:T(8,128)(2,1)}, u32[]{:S(2)}) copy-start(bf16[128,1024]{1,0:T(8,128)(2,1)} %rows.1) | copy-start | bytes 786436
Sparse Core Ops, SparseCore 0:
  68.6 98.6 all-reduce.3

commit v3 on v2

--- a/solution.py
+++ b/solution.py
@@ -304,32 +304,20 @@
             copy.wait()
 
 
-def run_streams(streams):
+STEPS = [
+    ("pick", 0), ("forward_a", 0), ("pick", 1), ("pick", 2), ("other_z",), ("forward_b", 0),
+    ("pick", 4), ("far_a", 0), ("pick", 3), ("forward_b", 1), ("forward_b", 2), ("forward_a", 1),
+    ("pick", 5), ("pick", 6), ("forward_b", 4), ("forward_b", 3), ("far_a", 1), ("pick", 7),
+    ("forward_b", 5), ("forward_b", 6), ("forward_b", 7), ("finish",),
+]
+
+
+def stream_steps(streams):
     def do(name, *given):
         for stream in streams:
             getattr(stream, name)(*given)
 
-    do("pick", 0)
-    do("forward_a", 0)
-    do("pick", 1)
-    do("pick", 2)
-    do("other_z")
-    do("forward_b", 0)
-    do("pick", 4)
-    do("far_a", 0)
-    do("pick", 3)
-    do("forward_b", 1)
-    do("forward_b", 2)
-    do("forward_a", 1)
-    do("pick", 5)
-    do("pick", 6)
-    do("forward_b", 4)
-    do("forward_b", 3)
-    do("far_a", 1)
-    do("pick", 7)
-    for order in (5, 6, 7):
-        do("forward_b", order)
-    do("finish")
+    return [functools.partial(do, *step) for step in STEPS]
 
 
 def tell(links, flow, ids, value, out):
@@ -359,7 +347,8 @@
         stream.begin()
     for copy in told:
         copy.wait_recv()
-    run_streams(gathers + streams)
+    for step in stream_steps(gathers + streams):
+        step()
     links.finish()
 
 
@@ -388,35 +377,272 @@
     )(rows, slots, kv)
 
 
-def next_kernel(rows, table, got, tokens, out_buf, far_buf, send, recv):
+DISPATCH_SEMS = 2 * 49
+
+
+def dispatch_scratch():
+    return [
+        pltpu.VMEM((2, 4, 2, 8, CAP, WIDTH // 2), jnp.bfloat16),
+        pltpu.VMEM((2, 8, 2, CAP, WIDTH // 2), jnp.bfloat16),
+    ]
+
+
+def semaphores(count):
+    return [pltpu.SemaphoreType.DMA((count,)), pltpu.SemaphoreType.DMA((count,))]
+
+
+def share_small(links, part, got):
+    me = lax.axis_index("grp")
+    copies = [
+        links.start(part, got.at[me], i, "grp", (me + 1 + n) % 8)
+        for n, i in enumerate(links.ids(7))
+    ]
+    got[me] = part[...]
+    return copies
+
+
+def add_small(copies, got):
+    for copy in copies:
+        copy.wait_recv()
+    summed = got[0]
+    for i in range(1, 8):
+        summed = summed + got[i]
+    return summed
+
+
+def greet_both(seq_peers):
+    me = lax.axis_index("grp")
+    barrier = pltpu.get_barrier_semaphore()
+    for peer in seq_peers:
+        pl.semaphore_signal(barrier, inc=1, device_id={"seq": peer}, device_id_type=MESH)
+    for n in range(1, 8):
+        pl.semaphore_signal(
+            barrier, inc=1, device_id={"grp": (me + n) % 8}, device_id_type=MESH
+        )
+    pl.semaphore_wait(barrier, len(seq_peers) + 7)
+
+
+CHUNK = 32
+CHUNKS = 256 // CHUNK
+LINE_STEPS = CHUNKS + 12
+LINE_SEMS = 8 * CHUNKS
+
+
+class LineSum:
+    def __init__(self, links, part, total, held, sibling, arrived):
+        me = lax.axis_index("grp")
+        self.links, self.part, self.total = links, part, total
+        self.held, self.sibling, self.arrived = held, sibling, arrived
+        self.core, chip = me % 2, me // 2
+        high = chip // 2
+        self.depth = chip + high * (3 - 2 * chip)
+        self.twin = chip * 2 + 1 - self.core
+        self.inner = me + 2 - 4 * high
+        self.outer = (me + 6 + 4 * high) % 8
+        self.outgoing, self.incoming = 1 - high, high
+        self.pair_id, self.chain_id, self.spread_id, self.share_id = (
+            links.ids(2 * CHUNKS)[0] for _ in range(4)
+        )
+
+    def local(self, stream, i):
+        return pl.ds(pl.multiple_of(stream * 256 + i * CHUNK, CHUNK), CHUNK)
+
+    def whole(self, half, stream, i):
+        return pl.ds(pl.multiple_of(half * 512 + stream * 256 + i * CHUNK, CHUNK), CHUNK)
+
+    def pair(self, stream, i):
+        return self.links.copy(
+            self.part.at[self.whole(1 - self.core, stream, i)],
+            self.sibling.at[self.local(stream, i)],
+            self.pair_id + stream * CHUNKS + i,
+            "grp",
+            self.twin,
+        )
+
+    def chain(self, stream, i, peer):
+        spot = self.local(stream, i)
+        return self.links.copy(
+            self.held.at[spot],
+            self.arrived.at[spot],
+            self.chain_id + stream * CHUNKS + i,
+            "grp",
+            peer,
+        )
+
+    def spread(self, stream, i, peer):
+        spot = self.total.at[self.whole(self.core, stream, i)]
+        return self.links.copy(spot, spot, self.spread_id + stream * CHUNKS + i, "grp", peer)
+
+    def share(self, stream, i):
+        spot = self.total.at[self.whole(self.core, stream, i)]
+        return self.links.copy(spot, spot, self.share_id + stream * CHUNKS + i, "grp", self.twin)
+
+    def start_pair(self, i):
+        if i < CHUNKS:
+            self.pair(self.outgoing, i).start()
+            self.pair(self.incoming, i).start()
+
+    def begin(self):
+        for i in range(4):
+            self.start_pair(i)
+
+    def own_sum(self, stream, i):
+        self.pair(stream, i).wait_recv()
+        return self.part[self.whole(self.core, stream, i)].astype(jnp.float32) + self.sibling[
+            self.local(stream, i)
+        ].astype(jnp.float32)
+
+    def pass_on(self, stream, i, source, target):
+        own = self.own_sum(stream, i)
+        spot = self.local(stream, i)
+        self.chain(stream, i, source).wait_recv()
+        self.held[spot] = (own + self.arrived[spot].astype(jnp.float32)).astype(jnp.bfloat16)
+        self.chain(stream, i, target).start()
+
+    def hand_out(self, stream, i, source, target):
+        self.spread(stream, i, source).wait_recv()
+        self.spread(stream, i, target).start()
+        self.share(stream, i).start()
+
+    def step(self, t):
+        inner, outer = self.inner, self.outer
+
+        def at(lag):
+            return 0 <= t - lag < CHUNKS
+
+        if t < CHUNKS:
+            self.start_pair(t + 4)
+
+        @pl.when(self.depth == 0)
+        def _():
+            if at(0):
+                spot = self.local(self.outgoing, t)
+                self.held[spot] = self.own_sum(self.outgoing, t).astype(jnp.bfloat16)
+                self.chain(self.outgoing, t, inner).start()
+            if at(4):
+                i = t - 4
+                own = self.own_sum(self.incoming, i)
+                self.chain(self.incoming, i, inner).wait_recv()
+                self.total[self.whole(self.core, self.incoming, i)] = (
+                    own + self.arrived[self.local(self.incoming, i)].astype(jnp.float32)
+                ).astype(jnp.bfloat16)
+                self.spread(self.incoming, i, inner).start()
+                self.share(self.incoming, i).start()
+            if at(11):
+                self.spread(self.outgoing, t - 11, inner).wait_recv()
+                self.share(self.outgoing, t - 11).start()
+
+        @pl.when(self.depth == 1)
+        def _():
+            if at(0):
+                self.pass_on(self.outgoing, t, outer, inner)
+            if at(2):
+                self.pass_on(self.incoming, t - 2, inner, outer)
+            if at(6):
+                self.hand_out(self.incoming, t - 6, outer, inner)
+            if at(9):
+                self.hand_out(self.outgoing, t - 9, inner, outer)
+
+    def finish(self):
+        @pl.when(self.depth == 0)
+        def _():
+            for i in range(CHUNKS):
+                self.chain(self.outgoing, i, self.inner).wait_send()
+                self.spread(self.incoming, i, self.inner).wait_send()
+
+        @pl.when(self.depth == 1)
+        def _():
+            for i in range(CHUNKS):
+                self.chain(self.outgoing, i, self.inner).wait_send()
+                self.chain(self.incoming, i, self.outer).wait_send()
+                self.spread(self.incoming, i, self.inner).wait_send()
+                self.spread(self.outgoing, i, self.outer).wait_send()
+
+        for i in range(CHUNKS):
+            for stream in (0, 1):
+                self.pair(stream, i).wait_send()
+                self.share(stream, i).wait()
+
+
+def weave(line, steps):
+    placed = 0
+    for t in range(LINE_STEPS):
+        line.step(t)
+        due = len(steps) if t == LINE_STEPS - 1 else (t + 1) * len(steps) // LINE_STEPS
+        for step in steps[placed:due]:
+            step()
+        placed = due
+
+
+def rows_kernel(
+    rows, table, part, back_part, got, stats, back_total,
+    tokens, out_buf, far_buf, stats_got, held, sibling, arrived, send, recv,
+):
     flows = [Flow(0, WIDTH // 2), Flow(1, WIDTH // 2)]
     links = Links(send, recv)
-    greet("seq", near_peers(flows[0]))
+    line = LineSum(links, back_part, back_total, held, sibling, arrived)
+    greet_both(near_peers(flows[0]))
     streams = [
         DispatchStream(links, flow, rows, tokens, table, out_buf, far_buf, got) for flow in flows
     ]
     for stream in streams:
         stream.begin()
-    run_streams(streams)
+    copies = share_small(links, part, stats_got)
+    line.begin()
+    weave(line, stream_steps(streams))
+    stats[...] = add_small(copies, stats_got)
+    line.finish()
     links.finish()
 
 
-def dispatch_next(rows, table):
+def dispatch_rows(rows, table, part, back_part):
     return pl.pallas_call(
-        next_kernel,
+        rows_kernel,
         name="dispatch_rows",
-        out_shape=jax.ShapeDtypeStruct((2, 32, CAP, WIDTH), jnp.bfloat16),
+        out_shape=(
+            jax.ShapeDtypeStruct((2, 32, CAP, WIDTH), jnp.bfloat16),
+            jax.ShapeDtypeStruct(part.shape, jnp.float32),
+            jax.ShapeDtypeStruct(back_part.shape, jnp.bfloat16),
+        ),
+        in_specs=[VMEM, VMEM, VMEM, VMEM],
+        out_specs=(ANY, VMEM, VMEM),
+        scratch_shapes=[pltpu.VMEM((2, 8, LEN, WIDTH // 2), jnp.bfloat16)]
+        + dispatch_scratch()
+        + [pltpu.VMEM((8,) + part.shape, jnp.float32)]
+        + [pltpu.VMEM((512, FF), jnp.bfloat16)] * 3
+        + semaphores(DISPATCH_SEMS + 7 + LINE_SEMS),
+        compiler_params=params(2),
+    )(rows, table, part, back_part)
+
+
+def line_kernel(part, squares, total, square_sum, held, sibling, arrived, small, send, recv):
+    links = Links(send, recv)
+    line = LineSum(links, part, total, held, sibling, arrived)
+    greet_both([])
+    line.begin()
+    copies = share_small(links, squares, small)
+    for t in range(LINE_STEPS):
+        line.step(t)
+    square_sum[...] = add_small(copies, small)
+    line.finish()
+    links.finish()
+
+
+def line_sum(part, squares):
+    return pl.pallas_call(
+        line_kernel,
+        name="line_sum",
+        out_shape=(
+            jax.ShapeDtypeStruct((1024, FF), jnp.bfloat16),
+            jax.ShapeDtypeStruct((8, LEN), jnp.float32),
+        ),
         in_specs=[VMEM, VMEM],
-        out_specs=ANY,
-        scratch_shapes=[
-            pltpu.VMEM((2, 8, LEN, WIDTH // 2), jnp.bfloat16),
-            pltpu.VMEM((2, 4, 2, 8, CAP, WIDTH // 2), jnp.bfloat16),
-            pltpu.VMEM((2, 8, 2, CAP, WIDTH // 2), jnp.bfloat16),
-            pltpu.SemaphoreType.DMA((98,)),
-            pltpu.SemaphoreType.DMA((98,)),
-        ],
-        compiler_params=params(2),
-    )(rows, table)
+        out_specs=(VMEM, VMEM),
+        scratch_shapes=[pltpu.VMEM((512, FF), jnp.bfloat16)] * 3
+        + [pltpu.VMEM((8, 8, LEN), jnp.float32)]
+        + semaphores(LINE_SEMS + 7),
+        compiler_params=params(3),
+    )(part, squares)
 
 
 BACK_SHIFTS = [2, 1, 3, 0]
@@ -550,80 +776,81 @@
     told = []
     for flow in flows:
         told += tell(links, flow, links.ids(7), gates, gates_all.at[flow.which])
-    for order in range(8):
-        for stream in streams:
-            stream.begin(order)
+    turns = [(p * 4 + step, t) for p in (0, 1) for t in (0, 1) for step in range(4)]
+    for order, t in turns:
+        for pair in pairs:
+            pair[t].begin(order)
     for copy in told:
         copy.wait_recv()
     codes = [flow.codes() for flow in flows]
     g_id = [links.ids(8), links.ids(8)]
     grads_sent = []
-
-    def do(name, *given):
-        for stream in streams:
-            getattr(stream, name)(*given)
-
-    def combine(order):
-        for flow in flows:
-            k = flow.which
-            forward, backward = pairs[k]
-            block = forward.block(order)
+    mixes = {}
+
+    def mix_of(flow, order):
+        k = flow.which
+        if (k, order) not in mixes:
+            block = pairs[k][0].block(order)
             ids, weight = table[k, block], gates_all[k, block]
             mix = jnp.zeros((LEN, LEN), jnp.float32)
             for c in range(TOP):
                 mix = mix + jnp.where(ids[c : c + 1, :] == codes[k], weight[c : c + 1, :], 0.0)
-            mix = mix.astype(jnp.bfloat16)
-            for stream in (forward, backward):
-                rows = stream.arrive(order)
-                summed = lax.dot_general(
-                    mix, rows, (((0,), (0,)), ((), ())), preferred_element_type=jnp.float32
+            mixes[k, order] = mix.astype(jnp.bfloat16)
+        return mixes[k, order]
+
+    def combine(order, t):
+        for flow in flows:
+            k = flow.which
+            stream = pairs[k][t]
+            mix = mix_of(flow, order)
+            rows = stream.arrive(order)
+            summed = lax.dot_general(
+                mix, rows, (((0,), (0,)), ((), ())), preferred_element_type=jnp.float32
+            )
+            stream.add_on(order, summed)
+            if t == 1:
+                continue
+            block = stream.block(order)
+            ids = table[k, block]
+            dots = lax.dot_general(
+                rows,
+                tokens[k, block],
+                (((1,), (1,)), ((), ())),
+                preferred_element_type=jnp.float32,
+            )
+            for c in range(TOP):
+                grad_part[k, order, c : c + 1, :] = jnp.sum(
+                    jnp.where(ids[c : c + 1, :] == codes[k], dots, 0.0), axis=0, keepdims=True
                 )
-                stream.add_on(order, summed)
-                if stream is backward:
-                    continue
-                dots = lax.dot_general(
-                    rows,
-                    tokens[k, block],
-                    (((1,), (1,)), ((), ())),
-                    preferred_element_type=jnp.float32,
+            grad_part[k, order, TOP:, :] = jnp.zeros((8 - TOP, LEN), jnp.float32)
+            if order < 7:
+                peer = flow.at(z=stream.zs[order // 4], da=BACK_SHIFTS[order % 4])
+                grads_sent.append(
+                    links.start(
+                        grad_part.at[k, order],
+                        grad_got.at[k, order],
+                        g_id[k][order],
+                        "seq",
+                        peer,
+                    )
                 )
-                for c in range(TOP):
-                    grad_part[k, order, c : c + 1, :] = jnp.sum(
-                        jnp.where(ids[c : c + 1, :] == codes[k], dots, 0.0),
-                        axis=0,
-                        keepdims=True,
-                    )
-                grad_part[k, order, TOP:, :] = jnp.zeros((8 - TOP, LEN), jnp.float32)
-                if order < 7:
-                    peer = flow.at(z=forward.zs[order // 4], da=BACK_SHIFTS[order % 4])
-                    grads_sent.append(
-                        links.start(
-                            grad_part.at[k, order],
-                            grad_got.at[k, order],
-                            g_id[k][order],
-                            "seq",
-                            peer,
-                        )
-                    )
-
-    do("forward_b", 0)
-    do("forward_b", 1)
-    combine(0)
-    do("forward_b", 2)
-    combine(1)
-    do("forward_b", 3)
-    combine(2)
-    do("forward_b", 4)
-    combine(3)
-    do("forward_b", 5)
-    combine(4)
-    do("send_z")
-    do("forward_b", 6)
-    do("forward_b", 7)
-    combine(5)
-    combine(6)
-    combine(7)
-    do("finish")
+
+    def forward(index):
+        if index < len(turns):
+            order, t = turns[index]
+            for pair in pairs:
+                pair[t].forward_b(order)
+
+    forward(0)
+    forward(1)
+    for index, (order, t) in enumerate(turns):
+        forward(index + 2)
+        combine(order, t)
+        if index in (5, 9):
+            for pair in pairs:
+                pair[(index - 5) // 4].send_z()
+    for stream in streams:
+        stream.finish()
     gathered = grad_part[0, 7] + grad_part[1, 7]
     for copy in grads_sent:
         copy.wait_recv()
@@ -662,7 +889,7 @@
             pltpu.SemaphoreType.DMA((COLLECT_SEMS,)),
             pltpu.SemaphoreType.DMA((COLLECT_SEMS,)),
         ],
-        compiler_params=params(3),
+        compiler_params=params(4),
     )(results, back_results, table, gates, tokens)
 
 
@@ -699,145 +926,6 @@
             pltpu.SemaphoreType.DMA((7,)),
         ],
         compiler_params=params(collective_id),
-    )(part)
-
-
-CHUNK = 32
-CHUNKS = 256 // CHUNK
-
-
-def hidden_kernel(part, total, held, sibling, arrived, send, recv):
-    me = lax.axis_index("grp")
-    core, chip = me % 2, me // 2
-    high = chip // 2
-    depth = chip + high * (3 - 2 * chip)
-    twin = chip * 2 + 1 - core
-    inner = me + 2 - 4 * high
-    outer = (me + 6 + 4 * high) % 8
-    links = Links(send, recv)
-    pair_id, chain_id, spread_id, share_id = (links.ids(2 * CHUNKS) for _ in range(4))
-    outgoing, incoming = 1 - high, high
-    barrier = pltpu.get_barrier_semaphore()
-    for peer in (twin, inner):
-        pl.semaphore_signal(barrier, inc=1, device_id={"grp": peer}, device_id_type=MESH)
-
-    @pl.when(depth == 1)
-    def _():
-        pl.semaphore_signal(barrier, inc=1, device_id={"grp": outer}, device_id_type=MESH)
-        pl.semaphore_wait(barrier, 3)
-
-    @pl.when(depth == 0)
-    def _():
-        pl.semaphore_wait(barrier, 2)
-
-    def local(stream, i):
-        return pl.ds(pl.multiple_of(stream * 256 + i * CHUNK, CHUNK), CHUNK)
-
-    def whole(half, stream, i):
-        return pl.ds(pl.multiple_of(half * 512 + stream * 256 + i * CHUNK, CHUNK), CHUNK)
-
-    def pair(stream, i):
-        return links.copy(
-            part.at[whole(1 - core, stream, i)],
-            sibling.at[local(stream, i)],
-            pair_id[0] + stream * CHUNKS + i,
-            "grp",
-            twin,
-        )
-
-    def chain(stream, i, peer):
-        spot = local(stream, i)
-        return links.copy(
-            held.at[spot], arrived.at[spot], chain_id[0] + stream * CHUNKS + i, "grp", peer
-        )
-
-    def spread(stream, i, peer):
-        spot = total.at[whole(core, stream, i)]
-        return links.copy(spot, spot, spread_id[0] + stream * CHUNKS + i, "grp", peer)
-
-    def share(stream, i):
-        spot = total.at[whole(core, stream, i)]
-        return links.copy(spot, spot, share_id[0] + stream * CHUNKS + i, "grp", twin)
-
-    for i in range(CHUNKS):
-        pair(outgoing, i).start()
-        pair(incoming, i).start()
-
-    def own_sum(stream, i):
-        pair(stream, i).wait_recv()
-        return part[whole(core, stream, i)].astype(jnp.float32) + sibling[
-            local(stream, i)
-        ].astype(jnp.float32)
-
-    @pl.when(depth == 0)
-    def _():
-        for i in range(CHUNKS):
-            held[local(outgoing, i)] = own_sum(outgoing, i).astype(jnp.bfloat16)
-            chain(outgoing, i, inner).start()
-        for i in range(CHUNKS):
-            own = own_sum(incoming, i)
-            chain(incoming, i, inner).wait_recv()
-            total[whole(core, incoming, i)] = (
-                own + arrived[local(incoming, i)].astype(jnp.float32)
-            ).astype(jnp.bfloat16)
-            spread(incoming, i, inner).start()
-            share(incoming, i).start()
-        for i in range(CHUNKS):
-            spread(outgoing, i, inner).wait_recv()
-            share(outgoing, i).start()
-        for i in range(CHUNKS):
-            chain(outgoing, i, inner).wait_send()
-            spread(incoming, i, inner).wait_send()
-
-    @pl.when(depth == 1)
-    def _():
-        def pass_on(stream, i, source, target):
-            own = own_sum(stream, i)
-            chain(stream, i, source).wait_recv()
-            held[local(stream, i)] = (
-                own + arrived[local(stream, i)].astype(jnp.float32)
-            ).astype(jnp.bfloat16)
-            chain(stream, i, target).start()
-
-        def hand_out(stream, i, source, target):
-            spread(stream, i, source).wait_recv()
-            spread(stream, i, target).start()
-            share(stream, i).start()
-
-        for i in range(CHUNKS):
-            pass_on(outgoing, i, outer, inner)
-            pass_on(incoming, i, inner, outer)
-        for i in range(CHUNKS):
-            hand_out(incoming, i, outer, inner)
-            hand_out(outgoing, i, inner, outer)
-        for i in range(CHUNKS):
-            chain(outgoing, i, inner).wait_send()
-            chain(incoming, i, outer).wait_send()
-            spread(incoming, i, inner).wait_send()
-            spread(outgoing, i, outer).wait_send()
-
-    for i in range(CHUNKS):
-        for stream in (0, 1):
-            pair(stream, i).wait_send()
-            share(stream, i).wait()
-
-
-def hidden_sum(part):
-    sems = 8 * CHUNKS
-    return pl.pallas_call(
-        hidden_kernel,
-        name="hidden_sum",
-        out_shape=jax.ShapeDtypeStruct((1024, FF), jnp.bfloat16),
-        in_specs=[VMEM],
-        out_specs=VMEM,
-        scratch_shapes=[
-            pltpu.VMEM((512, FF), jnp.bfloat16),
-            pltpu.VMEM((512, FF), jnp.bfloat16),
-            pltpu.VMEM((512, FF), jnp.bfloat16),
-            pltpu.SemaphoreType.DMA((sems,)),
-            pltpu.SemaphoreType.DMA((sems,)),
-        ],
-        compiler_params=params(5),
     )(part)
 
 
@@ -946,9 +1034,51 @@
     )(rows, weight)
 
 
-def expert_kernel(pre, act_grad, w_out, w_in, out, grad):
+def row_product_kernel(rows, gain, weight, out, squares):
+    wide = rows[0].astype(jnp.float32)
+    out[0] = jnp.dot(
+        (wide * gain[...]).astype(jnp.bfloat16), weight[0], preferred_element_type=jnp.float32
+    ).astype(jnp.bfloat16)
+    squares[0] = lax.dot_general(
+        jnp.ones((8, WIDTH), jnp.float32),
+        wide * wide,
+        (((1,), (1,)), ((), ())),
+        precision=lax.Precision.HIGHEST,
+        preferred_element_type=jnp.float32,
+    )
+
+
+def row_product(rows, gain, weight):
+    sets, count, depth = rows.shape
+    return pl.pallas_call(
+        row_product_kernel,
+        name="row_product",
+        grid=(sets,),
+        out_shape=(
+            jax.ShapeDtypeStruct((sets, count, FF), jnp.bfloat16),
+            jax.ShapeDtypeStruct((sets, 8, count), jnp.float32),
+        ),
+        in_specs=[
+            pl.BlockSpec((1, count, depth), lambda m: (m, 0, 0)),
+            pl.BlockSpec((1, depth), lambda m: (0, 0)),
+            pl.BlockSpec((1,) + weight.shape[1:], lambda m: (m, 0, 0)),
+        ],
+        out_specs=(
+            pl.BlockSpec((1, count, FF), lambda m: (m, 0, 0)),
+            pl.BlockSpec((1, 8, count), lambda m: (m, 0, 0)),
+        ),
+        compiler_params=params(),
+        cost_estimate=pl.CostEstimate(
+            flops=2 * sets * count * depth * FF,
+            bytes_accessed=2 * sets * (count * depth + depth * FF + count * FF),
+            transcendentals=0,
+        ),
+    )(rows, gain[None, :], weight)
+
+
+def expert_kernel(pre, inverse, act_grad, w_out, w_in, out, grad):
     root = 0.7978845608028654
-    wide = pre[0].astype(jnp.float32)
+    wide = pre[0].astype(jnp.float32) * inverse[0]
     square = wide * wide
     curve = jnp.tanh(root * wide * (1.0 + 0.044715 * square))
     active = (0.5 * wide * (1.0 + curve)).astype(jnp.bfloat16)
@@ -962,7 +1092,7 @@
     ).astype(jnp.bfloat16)
 
 
-def expert_products(pre, act_grad, w_out, w_in):
+def expert_products(pre, inverse, act_grad, w_out, w_in):
     sets, count, _ = pre.shape
     tile = 256
 
@@ -978,7 +1108,7 @@
         name="expert_products",
         grid=(sets, count // tile),
         out_shape=(shape, shape),
-        in_specs=[moving(FF), moving(FF), held(w_out), held(w_in)],
+        in_specs=[moving(FF), moving(1), moving(FF), held(w_out), held(w_in)],
         out_specs=(moving(WIDTH), moving(WIDTH)),
         compiler_params=params(),
         cost_estimate=pl.CostEstimate(
@@ -986,7 +1116,7 @@
             bytes_accessed=4 * sets * (count * (FF + WIDTH) + FF * WIDTH),
             transcendentals=sets * count * FF,
         ),
-    )(pre, act_grad, w_out, w_in)
+    )(pre, inverse, act_grad, w_out, w_in)
 
 
 def body(
@@ -1026,11 +1156,10 @@
     got_grads, tokens_grad, table, kv = dispatch_first(
         grad_out, slots, jnp.concatenate([key_states, value_states], axis=1)
     )
-    partial_back = product(
-        got_grads.reshape(2, experts * CAP, width), w_out_local, True, "back_product"
-    )
-    act_grad = lax.psum(partial_back, "grp")
-
+    entries_all = experts * CAP
+    back_part = product(
+        got_grads.reshape(2, entries_all, width), w_out_local, True, "back_product"
+    )
     resid_state = attend(query_states, kv.reshape(experts * length, 2 * HEAD_DIM), doc_ids, inputs)
     state_wide = resid_state.astype(jnp.float32)
     scaled = state_wide * norm_gain[None, :]
@@ -1041,30 +1170,33 @@
         preferred_element_type=jnp.float32,
     )
     square_part = jnp.sum(state_wide * state_wide, axis=1)[None, :]
-    stats = small_sum(
+    got_rows, stats, act_grad = dispatch_rows(
+        resid_state,
+        table,
         jnp.concatenate([raw_part, square_part, jnp.zeros((7, length), jnp.float32)], axis=0),
-        6,
-        "sum_stats",
+        back_part.reshape(2 * entries_all, FF),
     )
     inv_row = lax.rsqrt(stats[2 * experts] / D + eps_norm)
     inv_rms = inv_row[:, None]
     raw_logits = stats[: 2 * experts].T
     logits = raw_logits * inv_rms
-    normed = (scaled * inv_rms).astype(jnp.bfloat16)
     chosen = jnp.sum(jnp.where(one_hot, logits[:, None, :], 0.0), axis=2)
     lifted = jax.nn.sigmoid(chosen)
     denominator = gate_offset + jnp.sum(kept_wide * lifted, axis=1, keepdims=True)
     gates = kept_wide * lifted / denominator
     gates_t = jnp.concatenate([gates.T, jnp.zeros((8 - TOP, length), jnp.float32)], axis=0)
 
-    got_rows = dispatch_next(normed, table)
-    partial_value = product(
-        got_rows.reshape(2, experts * CAP, width), w_in_local, False, "row_product"
-    )
-    pre_act = hidden_sum(partial_value.reshape(2 * experts * CAP, FF)).reshape(
-        2, experts * CAP, FF
-    )
-    expert_out, entry_grad = expert_products(pre_act, act_grad, w_out_local, w_in_local)
+    row_part, squares = row_product(
+        got_rows.reshape(2, entries_all, width), norm_gain, w_in_local
+    )
+    pre_act, square_sum = line_sum(
+        row_part.reshape(2 * entries_all, FF), squares[:, 0].reshape(8, LEN)
+    )
+    pre_act = pre_act.reshape(2, entries_all, FF)
+    inverse = lax.rsqrt(square_sum / D + eps_norm).reshape(2, entries_all, 1)
+    expert_out, entry_grad = expert_products(
+        pre_act, inverse, act_grad.reshape(2, entries_all, FF), w_out_local, w_in_local
+    )
     mixture, entry_sum, gate_part = collect(
         expert_out.reshape(2, experts, CAP, width),
         entry_grad.reshape(2, experts, CAP, width),

time: 353 us -> 345 us (0.977)
  between operations: 17.5 us -> 4.12 us
  Pallas kernels: 312 us -> 317 us
    pallas_call x2 -> x3, Pallas kernels: 132 us -> 163 us  [the longest x1 93.3 us: dispatch_rows(): pl.pallas_call(rows_kernel, name='dispatch_rows', out_shape=(jax.ShapeDty...]
    pallas_call x2 -> x1, Pallas kernels: 26.9 us -> 12.3 us  [small_sum(): pl.pallas_call(small_sum_kernel, name=name, out_shape=jax.ShapeDtypeStruc...]
    pallas_call x2 -> x1, Pallas kernels: 13.9 us -> 6.91 us  [product(): pl.pallas_call(functools.partial(product_kernel, turned), name=name, grid...]
    pallas_call x1, Pallas kernels: 69.6 us -> 64.7 us  [collect(): pl.pallas_call(collect_kernel, name='collect', out_shape=(jax.ShapeDtypeS...]
  transfers between devices with their start and end apart: 1 -> 0, of which waited for: 0 -> 0; matrix products, arithmetic and copies ran while one was open for 3% -> 0% of each run, Pallas kernels for 47% -> 0%
where the time goes in v3:
time: 345 us; the launch traced here: 344 us
  Pallas kernels  317 us (92%)
  other arithmetic  13.2 us (4%)
  local copies, waits for them, and re-layouts  6.71 us (2%)
  between operations  4.12 us (1%)
  matrix products  3.76 us (1%)
    pallas_call x1, Pallas kernels, dispatch_rows(): pl.pallas_call(rows_kernel, name='dispatch_rows', out_shape=(jax.ShapeDty...  93.3 us
    pallas_call x1, Pallas kernels, collect(): pl.pallas_call(collect_kernel, name='collect', out_shape=(jax.ShapeDtypeS...  64.7 us
    pallas_call x1, Pallas kernels, line_sum(): pl.pallas_call(line_kernel, name='line_sum', out_shape=(jax.ShapeDtypeStr...  60.2 us
    pallas_call x1, Pallas kernels, dispatch_first(): pl.pallas_call(first_kernel, name='dispatch_grads', out_shape=(jax.ShapeD...  49.8 us
    pallas_call x1, Pallas kernels, expert_products(): pl.pallas_call(expert_kernel, name='expert_products', grid=(sets, count /...  14.2 us
    pallas_call x1, Pallas kernels, small_sum(): pl.pallas_call(small_sum_kernel, name=name, out_shape=jax.ShapeDtypeStruc...  12.3 us
    pallas_call x1, Pallas kernels, row_product(): pl.pallas_call(row_product_kernel, name='row_product', grid=(sets,), out_...  9.5 us
    pallas_call x1, Pallas kernels, product(): pl.pallas_call(functools.partial(product_kernel, turned), name=name, grid...  6.91 us

profile of v3, /device:TPU:1, one launch (start us, length us, event | category | flops | bytes accessed | tf_op | source)
XLA Modules:
  0.0 344.4 jit_solution(8683682036137791824)
XLA Ops:
  0.6 0.0 copy-start
  0.7 0.8 dynamic_slice.3
  1.5 1.1 convert_reduce_fusion
  2.5 0.7 fusion.26
  6.5 0.6 pad_add_fusion.bounds
  7.1 0.7 broadcast_multiply_fusion
  7.8 0.7 select_add_fusion
  8.4 0.1 copy.28
  8.6 0.1 eq.30
  8.7 0.1 copy.29
  8.8 0.1 and.37
  8.9 0.3 fusion.4
  9.2 0.0 copy-start.4
  9.3 0.1 convert_element_type.38
  9.4 0.1 copy.30
  9.4 0.6 concatenate.12.slots
  10.1 1.4 pad_maximum_fusion.kv_in
  11.5 49.8 %dispatch_grads.1 = (bf16[2,32,16,1024]{3,2,1,0:T(8,128)(2,1)}, bf16[2,8,128,512]{3,2,1,0:T(8,128)(2,1)}, s32[2,8,8,128]{3,2,1,0:T(8,128)}, bf16[32,128,256]{2,1,0:T(8,128)(2,1)}) custom-call(bf16[128,1024]{1,0:T(8,128)(2,1)} %rows.1, s32[8,128]{1,0:T(8,128)} %concatenate.12.slots, bf16[128,256]{1,0:T(8,128)(2,1)} %pad_maximum_fusion.kv_in), custom_call_target="tpu_custom_call" | custom-call | tf_op jit(solution)/shard_map/dispatch_grads/pallas_call | solution.py:359
  61.3 0.7 copy.31.first_key
  62.0 0.6 iota_add_fusion.query_pos
  62.7 5.7 %attend.1.rows = bf16[128,1024]{1,0:T(8,128)(2,1)} custom-call(s32[4]{0:T(128)} %pad_add_fusion.bounds, bf16[128,1024]{1,0:T(8,128)(2,1)} %query.1, bf16[4096,256]{1,0:T(8,128)(2,1)} %bitcast.51, s32[128,1]{1,0:T(8,128)} %copy.31.first_key, s32[128,1]{1,0:T(8,128)} %iota_add_fusion.query_pos, bf16[128,1024]{1,0:T(8,128)(2,1)} %inputs.1), custom_call_target="tpu_custom_call" | custom-call | tf_op jit(solution)/shard_map/attend/pallas_call | solution.py:991
  68.4 1.1 fusion.8
  69.5 0.0 copy-done
  69.5 0.0 copy-done.4
  69.5 1.2 convolution_bitcast_fusion
  70.7 0.1 pad.4.clone
  70.8 0.7 maximum_maximum_fusion.part
  71.5 6.9 %back_product.1 = bf16[2,512,1408]{2,1,0:T(8,128)(2,1)} custom-call(bf16[2,512,1024]{2,1,0:T(8,128)(2,1)} %bitcast.64, bf16[2,1408,1024]{2,1,0:T(8,128)(2,1)} %bitcast.58), custom_call_target="tpu_custom_call" | custom-call | flops 2952790016 | bytes 10747904 | tf_op jit(solution)/shard_map/back_product/pallas_call | solution.py:1018
  78.4 93.3 %dispatch_rows.1 = (bf16[2,32,16,1024]{3,2,1,0:T(8,128)(2,1)}, f32[72,128]{1,0:T(8,128)}, bf16[1024,1408]{1,0:T(8,128)(2,1)}) custom-call(bf16[128,1024]{1,0:T(8,128)(2,1)} %attend.1.rows, s32[2,8,8,128]{3,2,1,0:T(8,128)} %get-tuple-element.19.table, f32[72,128]{1,0:T(8,128)} %maximum_maximum_fusion.part, bf16[1024,1408]{1,0:T(8,128)(2,1)} %bitcast.50), custom_call_target="tpu_custom_call" | custom-call | tf_op jit(solution)/shard_map/dispatch_rows/pallas_call | solution.py:599
  171.7 9.5 %row_product.1 = (bf16[2,512,1408]{2,1,0:T(8,128)(2,1)}, f32[2,8,512]{2,1,0:T(8,128)}) custom-call(bf16[2,512,1024]{2,1,0:T(8,128)(2,1)} %bitcast.65, f32[1,1024]{1,0:T(1,128)} %bitcast.54, bf16[2,1024,1408]{2,1,0:T(8,128)(2,1)} %bitcast.60), custom_call_target="tpu_custom_call" | custom-call | flops 2952790016 | bytes 10747904 | tf_op jit(solution)/shard_map/row_product/pallas_call | solution.py:1053
  181.2 1.4 slice.25
  182.5 60.2 %line_sum.1 = (bf16[1024,1408]{1,0:T(8,128)(2,1)}, f32[8,128]{1,0:T(8,128)}) custom-call(bf16[1024,1408]{1,0:T(8,128)(2,1)} %bitcast.49, f32[8,128]{1,0:T(8,128)} %bitcast.55), custom_call_target="tpu_custom_call" | custom-call | tf_op jit(solution)/shard_map/line_sum/pallas_call | solution.py:632
  242.8 0.7 add_rsqrt_fusion
  243.4 1.2 reshape.115.inverse
  244.6 0.0 copy-start.3
  244.6 14.2 %expert_products.1 = (bf16[2,512,1024]{2,1,0:T(8,128)(2,1)}, bf16[2,512,1024]{2,1,0:T(8,128)(2,1)}) custom-call(bf16[2,512,1408]{2,1,0:T(8,128)(2,1)} %bitcast.63, f32[2,512,1]{2,1,0:T(8,128)} %reshape.115.inverse, bf16[2,512,1408]{2,1,0:T(8,128)(2,1)} %bitcast.62, bf16[2,1408,1024]{2,1,0:T(8,128)(2,1)} %bitcast.59, bf16[2,1024,1408]{2,1,0:T(8,128)(2,1)} %bitcast.61), custom_call_target="tpu_custom_call" | custom-call | flops 5905580032 | bytes 21495808 | tf_op jit(solution)/shard_map/expert_products/pallas_call | solution.py:1106
  258.8 0.0 copy-done.3
  258.9 0.6 concatenate.15.gates
  259.6 0.0 copy-start.1
  259.6 0.0 copy-start.5
  259.6 0.0 copy-start.2
  259.6 64.7 %collect.1 = (f32[128,1024]{1,0:T(8,128)}, f32[128,1024]{1,0:T(8,128)}, f32[8,128]{1,0:T(8,128)}) custom-call(bf16[2,32,16,1024]{3,2,1,0:T(8,128)(2,1)} %bitcast.52, bf16[2,32,16,1024]{3,2,1,0:T(8,128)(2,1)} %bitcast.53, s32[2,8,8,128]{3,2,1,0:T(8,128)} %get-tuple-element.19.table, f32[8,128]{1,0:T(8,128)} %concatenate.15.gates, ...), custom_call_target="tpu_custom_call" | custom-call | tf_op jit(solution)/shard_map/collect/pallas_call | solution.py:869
  324.2 0.0 copy-done.1
  324.3 0.0 copy-done.5
  324.3 2.0 fusion.7
  326.3 1.3 broadcast_select_fusion.part
  327.6 12.3 %sum_ends.1 = f32[8,128]{1,0:T(8,128)} custom-call(f32[8,128]{1,0:T(8,128)} %broadcast_select_fusion.part), custom_call_target="tpu_custom_call" | custom-call | tf_op jit(solution)/shard_map/sum_ends/pallas_call | solution.py:917
  340.0 0.7 fusion.21
  340.7 0.7 fusion.20
  341.4 0.7 bitcast_add_fusion
  342.1 0.0 copy-done.2
  342.1 2.3 fusion.3
  (12 shorter events, 0.2 us)
Async XLA Ops:
  0.6 68.9 %copy-start = (bf16[1024,64]{0,1:T(8,128)(2,1)S(1)}, bf16[1024,64]{0,1:T(8,128)(2,1)}, u32[]{:S(2)}) copy-start(bf16[1024,64]{0,1:T(8,128)(2,1)} %param.20) | copy-start | bytes 393220
  9.2 60.3 %copy-start.4 = (f32[1024]{0:T(1024)S(1)}, f32[1024]{0:T(1024)}, u32[]{:S(2)}) copy-start(f32[1024]{0:T(1024)} %param.19) | copy-start | bytes 12292
  244.6 14.2 %copy-start.3 = (f32[72,128]{1,0:T(8,128)S(1)}, f32[72,128]{1,0:T(8,128)}, u32[]{:S(2)}) copy-start(f32[72,128]{1,0:T(8,128)} %get-tuple-element.29) | copy-start | bytes 110596
  259.6 64.7 %copy-start.1 = (bf16[128,1024]{1,0:T(8,128)(2,1)S(1)}, bf16[128,1024]{1,0:T(8,128)(2,1)}, u32[]{:S(2)}) copy-start(bf16[128,1024]{1,0:T(8,128)(2,1)} %attend.1.rows) | copy-start | bytes 786436
  259.6 64.7 %copy-start.5 = (f32[1024]{0:T(1024)S(1)}, f32[1024]{0:T(1024)}, u32[]{:S(2)}) copy-start(f32[1024]{0:T(1024)} %param.19) | copy-start | bytes 12292
  259.6 82.6 %copy-start.2 = (bf16[128,1024]{1,0:T(8,128)(2,1)S(1)}, bf16[128,1024]{1,0:T(8,128)(2,1)}, u32[]{:S(2)}) copy-start(bf16[128,1024]{1,0:T(8,128)(2,1)} %rows.1) | copy-start | bytes 786436

commit v4 on v3

--- a/solution.py
+++ b/solution.py
@@ -424,13 +424,16 @@
 
 CHUNK = 32
 CHUNKS = 256 // CHUNK
-LINE_STEPS = CHUNKS + 12
+LINE_STEPS = CHUNKS + 13
+CLOSE_LAGS = (0, 2, 4, 6, 9, 11)
+WIDE_LAGS = (2, 4, 6, 8, 10, 12)
 LINE_SEMS = 8 * CHUNKS
 
 
 class LineSum:
-    def __init__(self, links, part, total, held, sibling, arrived):
+    def __init__(self, links, part, total, held, sibling, arrived, lags):
         me = lax.axis_index("grp")
+        self.lags = lags
         self.links, self.part, self.total = links, part, total
         self.held, self.sibling, self.arrived = held, sibling, arrived
         self.core, chip = me % 2, me // 2
@@ -506,6 +509,7 @@
 
     def step(self, t):
         inner, outer = self.inner, self.outer
+        pass_out, pass_in, end, hand_in, hand_back, last = self.lags
 
         def at(lag):
             return 0 <= t - lag < CHUNKS
@@ -519,8 +523,8 @@
                 spot = self.local(self.outgoing, t)
                 self.held[spot] = self.own_sum(self.outgoing, t).astype(jnp.bfloat16)
                 self.chain(self.outgoing, t, inner).start()
-            if at(4):
-                i = t - 4
+            if at(end):
+                i = t - end
                 own = self.own_sum(self.incoming, i)
                 self.chain(self.incoming, i, inner).wait_recv()
                 self.total[self.whole(self.core, self.incoming, i)] = (
@@ -528,20 +532,20 @@
                 ).astype(jnp.bfloat16)
                 self.spread(self.incoming, i, inner).start()
                 self.share(self.incoming, i).start()
-            if at(11):
-                self.spread(self.outgoing, t - 11, inner).wait_recv()
-                self.share(self.outgoing, t - 11).start()
+            if at(last):
+                self.spread(self.outgoing, t - last, inner).wait_recv()
+                self.share(self.outgoing, t - last).start()
 
         @pl.when(self.depth == 1)
         def _():
-            if at(0):
-                self.pass_on(self.outgoing, t, outer, inner)
-            if at(2):
-                self.pass_on(self.incoming, t - 2, inner, outer)
-            if at(6):
-                self.hand_out(self.incoming, t - 6, outer, inner)
-            if at(9):
-                self.hand_out(self.outgoing, t - 9, inner, outer)
+            if at(pass_out):
+                self.pass_on(self.outgoing, t - pass_out, outer, inner)
+            if at(pass_in):
+                self.pass_on(self.incoming, t - pass_in, inner, outer)
+            if at(hand_in):
+                self.hand_out(self.incoming, t - hand_in, outer, inner)
+            if at(hand_back):
+                self.hand_out(self.outgoing, t - hand_back, inner, outer)
 
     def finish(self):
         @pl.when(self.depth == 0)
@@ -580,7 +584,7 @@
 ):
     flows = [Flow(0, WIDTH // 2), Flow(1, WIDTH // 2)]
     links = Links(send, recv)
-    line = LineSum(links, back_part, back_total, held, sibling, arrived)
+    line = LineSum(links, back_part, back_total, held, sibling, arrived, WIDE_LAGS)
     greet_both(near_peers(flows[0]))
     streams = [
         DispatchStream(links, flow, rows, tokens, table, out_buf, far_buf, got) for flow in flows
@@ -617,7 +621,7 @@
 
 def line_kernel(part, squares, total, square_sum, held, sibling, arrived, small, send, recv):
     links = Links(send, recv)
-    line = LineSum(links, part, total, held, sibling, arrived)
+    line = LineSum(links, part, total, held, sibling, arrived, CLOSE_LAGS)
     greet_both([])
     line.begin()
     copies = share_small(links, squares, small)
@@ -932,7 +936,7 @@
 KEYS = 512
 
 
-def attend_kernel(bounds, query, kv, first_key, query_pos, inputs, resid, best, total, acc):
+def attend_kernel(firsts, query, kv, first_key, query_pos, inputs, resid, best, total, acc):
     scale = HEAD_DIM ** (-0.5) * 1.4426950408889634
     groups = HEADS // KV_HEADS
     best[...] = jnp.full(best.shape, -1e30, jnp.float32)
@@ -966,9 +970,14 @@
             )
         return carry
 
-    lax.fori_loop(bounds[0], bounds[1], functools.partial(step, True), 0)
-    lax.fori_loop(bounds[1], bounds[2], functools.partial(step, False), 0)
-    lax.fori_loop(bounds[2], bounds[3], functools.partial(step, True), 0)
+    first_query = lax.axis_index("seq") * LEN
+    low = firsts[0] // KEYS
+    high = (first_query + LEN + KEYS - 1) // KEYS
+    full_low = jnp.minimum((firsts[LEN - 1] + KEYS - 1) // KEYS, high)
+    full_high = jnp.maximum((first_query + 1) // KEYS, full_low)
+    lax.fori_loop(low, full_low, functools.partial(step, True), 0)
+    lax.fori_loop(full_low, full_high, functools.partial(step, False), 0)
+    lax.fori_loop(full_high, high, functools.partial(step, True), 0)
     for h in range(groups):
         cols = slice(h * HEAD_DIM, (h + 1) * HEAD_DIM)
         attended = (acc[h] / total[h]).astype(jnp.bfloat16).astype(jnp.float32)
@@ -979,14 +988,8 @@
     first_query = lax.axis_index("seq") * LEN
     query_pos = first_query + jnp.arange(LEN, dtype=jnp.int32)
     query_doc = lax.dynamic_slice_in_dim(doc_ids, first_query, LEN)
-    first_key = jnp.sum(
-        (doc_ids[None, :] < query_doc[:, None]).astype(jnp.int32), axis=1, keepdims=True
-    )
-    low = first_key[0, 0] // KEYS
-    high = (first_query + LEN + KEYS - 1) // KEYS
-    full_low = jnp.minimum((first_key[LEN - 1, 0] + KEYS - 1) // KEYS, high)
-    full_high = jnp.maximum((first_query + 1) // KEYS, full_low)
-    bounds = jnp.stack([low, full_low, full_high, high])
+    firsts = jnp.sum((doc_ids[None, :] < query_doc[:, None]).astype(jnp.int32), axis=1)
+    first_key = firsts[:, None]
     groups = HEADS // KV_HEADS
     return pl.pallas_call(
         attend_kernel,
@@ -1000,7 +1003,7 @@
             pltpu.VMEM((groups, LEN, HEAD_DIM), jnp.float32),
         ],
         compiler_params=params(),
-    )(bounds.astype(jnp.int32), query, kv, first_key, query_pos[:, None], inputs)
+    )(firsts, query, kv, first_key, query_pos[:, None], inputs)
 
 
 def product_kernel(turned, rows, weight, out):

time: 345 us -> 337 us (0.977)
  Pallas kernels: 317 us -> 313 us
    pallas_call x1, Pallas kernels: 93.3 us -> 88.1 us  [dispatch_rows(): pl.pallas_call(rows_kernel, name='dispatch_rows', out_shape=(jax.ShapeDty...]
where the time goes in v4:
time: 337 us
  Pallas kernels  313 us (93%)
  other arithmetic  12.6 us (4%)
  local copies, waits for them, and re-layouts  6.04 us (2%)
  matrix products  3.75 us (1%)
    pallas_call x1, Pallas kernels, dispatch_rows(): pl.pallas_call(rows_kernel, name='dispatch_rows', out_shape=(jax.ShapeDty...  88.1 us
    pallas_call x1, Pallas kernels, collect(): pl.pallas_call(collect_kernel, name='collect', out_shape=(jax.ShapeDtypeS...  67.1 us
    pallas_call x1, Pallas kernels, line_sum(): pl.pallas_call(line_kernel, name='line_sum', out_shape=(jax.ShapeDtypeStr...  60.5 us
    pallas_call x1, Pallas kernels, dispatch_first(): pl.pallas_call(first_kernel, name='dispatch_grads', out_shape=(jax.ShapeD...  49.8 us
    pallas_call x1, Pallas kernels, expert_products(): pl.pallas_call(expert_kernel, name='expert_products', grid=(sets, count /...  14.2 us
    pallas_call x1, Pallas kernels, small_sum(): pl.pallas_call(small_sum_kernel, name=name, out_shape=jax.ShapeDtypeStruc...  11.5 us
    pallas_call x1, Pallas kernels, row_product(): pl.pallas_call(row_product_kernel, name='row_product', grid=(sets,), out_...  9.5 us
    pallas_call x1, Pallas kernels, product(): pl.pallas_call(functools.partial(product_kernel, turned), name=name, grid...  6.91 us

profile of v4, /device:TPU:1, one launch (start us, length us, event | category | flops | bytes accessed | tf_op | source)
XLA Modules:
  0.0 336.6 jit_solution(9442838578221839685)
XLA Ops:
  0.6 0.0 copy-start
  0.6 0.8 dynamic_slice.3
  1.4 1.1 convert_reduce_fusion.firsts
  2.5 0.0 copy-start.6
  2.5 0.7 broadcast_multiply_fusion
  3.2 0.7 select_add_fusion
  3.9 0.1 copy.28
  4.0 0.1 eq.30
  4.1 0.1 copy.29
  4.2 0.1 and.16
  4.4 0.3 fusion.4
  4.7 0.0 copy-start.4
  4.7 0.1 convert_element_type.38
  4.8 0.1 copy.30
  4.9 0.6 concatenate.12.slots
  5.5 1.4 pad_maximum_fusion.kv_in
  6.9 49.8 %dispatch_grads.1 = (bf16[2,32,16,1024]{3,2,1,0:T(8,128)(2,1)}, bf16[2,8,128,512]{3,2,1,0:T(8,128)(2,1)}, s32[2,8,8,128]{3,2,1,0:T(8,128)}, bf16[32,128,256]{2,1,0:T(8,128)(2,1)}) custom-call(bf16[128,1024]{1,0:T(8,128)(2,1)} %rows.1, s32[8,128]{1,0:T(8,128)} %concatenate.12.slots, bf16[128,256]{1,0:T(8,128)(2,1)} %pad_maximum_fusion.kv_in), custom_call_target="tpu_custom_call" | custom-call | tf_op jit(solution)/shard_map/dispatch_grads/pallas_call | solution.py:359
  56.7 0.7 copy.31.first_key
  57.5 0.6 iota_add_fusion.query_pos
  58.1 0.0 copy-done.6
  58.1 5.8 %attend.1.rows = bf16[128,1024]{1,0:T(8,128)(2,1)} custom-call(s32[128]{0:T(128)} %copy-done.6, bf16[128,1024]{1,0:T(8,128)(2,1)} %query.1, bf16[4096,256]{1,0:T(8,128)(2,1)} %bitcast.45, s32[128,1]{1,0:T(8,128)} %copy.31.first_key, s32[128,1]{1,0:T(8,128)} %iota_add_fusion.query_pos, bf16[128,1024]{1,0:T(8,128)(2,1)} %inputs.1), custom_call_target="tpu_custom_call" | custom-call | tf_op jit(solution)/shard_map/attend/pallas_call | solution.py:994
  63.9 1.1 fusion.8
  65.0 0.0 copy-done
  65.0 0.0 copy-done.4
  65.0 1.2 convolution_bitcast_fusion
  66.2 0.1 pad.4.clone
  66.2 0.7 maximum_maximum_fusion.part
  66.9 6.9 %back_product.1 = bf16[2,512,1408]{2,1,0:T(8,128)(2,1)} custom-call(bf16[2,512,1024]{2,1,0:T(8,128)(2,1)} %bitcast.58, bf16[2,1408,1024]{2,1,0:T(8,128)(2,1)} %bitcast.52), custom_call_target="tpu_custom_call" | custom-call | flops 2952790016 | bytes 10747904 | tf_op jit(solution)/shard_map/back_product/pallas_call | solution.py:1021
  73.8 88.1 %dispatch_rows.1 = (bf16[2,32,16,1024]{3,2,1,0:T(8,128)(2,1)}, f32[72,128]{1,0:T(8,128)}, bf16[1024,1408]{1,0:T(8,128)(2,1)}) custom-call(bf16[128,1024]{1,0:T(8,128)(2,1)} %attend.1.rows, s32[2,8,8,128]{3,2,1,0:T(8,128)} %get-tuple-element.19.table, f32[72,128]{1,0:T(8,128)} %maximum_maximum_fusion.part, bf16[1024,1408]{1,0:T(8,128)(2,1)} %bitcast.44), custom_call_target="tpu_custom_call" | custom-call | tf_op jit(solution)/shard_map/dispatch_rows/pallas_call | solution.py:603
  161.9 9.5 %row_product.1 = (bf16[2,512,1408]{2,1,0:T(8,128)(2,1)}, f32[2,8,512]{2,1,0:T(8,128)}) custom-call(bf16[2,512,1024]{2,1,0:T(8,128)(2,1)} %bitcast.59, f32[1,1024]{1,0:T(1,128)} %bitcast.48, bf16[2,1024,1408]{2,1,0:T(8,128)(2,1)} %bitcast.54), custom_call_target="tpu_custom_call" | custom-call | flops 2952790016 | bytes 10747904 | tf_op jit(solution)/shard_map/row_product/pallas_call | solution.py:1056
  171.4 1.4 slice.15
  172.8 60.5 %line_sum.1 = (bf16[1024,1408]{1,0:T(8,128)(2,1)}, f32[8,128]{1,0:T(8,128)}) custom-call(bf16[1024,1408]{1,0:T(8,128)(2,1)} %bitcast.43, f32[8,128]{1,0:T(8,128)} %bitcast.49), custom_call_target="tpu_custom_call" | custom-call | tf_op jit(solution)/shard_map/line_sum/pallas_call | solution.py:636
  233.3 0.7 add_rsqrt_fusion
  234.0 1.2 reshape.109.inverse
  235.2 0.0 copy-start.3
  235.2 14.2 %expert_products.1 = (bf16[2,512,1024]{2,1,0:T(8,128)(2,1)}, bf16[2,512,1024]{2,1,0:T(8,128)(2,1)}) custom-call(bf16[2,512,1408]{2,1,0:T(8,128)(2,1)} %bitcast.57, f32[2,512,1]{2,1,0:T(8,128)} %reshape.109.inverse, bf16[2,512,1408]{2,1,0:T(8,128)(2,1)} %bitcast.56, bf16[2,1408,1024]{2,1,0:T(8,128)(2,1)} %bitcast.53, bf16[2,1024,1408]{2,1,0:T(8,128)(2,1)} %bitcast.55), custom_call_target="tpu_custom_call" | custom-call | flops 5905580032 | bytes 21495808 | tf_op jit(solution)/shard_map/expert_products/pallas_call | solution.py:1109
  249.4 0.0 copy-done.3
  249.5 0.6 concatenate.15.gates
  250.1 0.0 copy-start.1
  250.1 0.0 copy-start.5
  250.1 0.0 copy-start.2
  250.2 67.1 %collect.1 = (f32[128,1024]{1,0:T(8,128)}, f32[128,1024]{1,0:T(8,128)}, f32[8,128]{1,0:T(8,128)}) custom-call(bf16[2,32,16,1024]{3,2,1,0:T(8,128)(2,1)} %bitcast.46, bf16[2,32,16,1024]{3,2,1,0:T(8,128)(2,1)} %bitcast.47, s32[2,8,8,128]{3,2,1,0:T(8,128)} %get-tuple-element.19.table, f32[8,128]{1,0:T(8,128)} %concatenate.15.gates, ...), custom_call_target="tpu_custom_call" | custom-call | tf_op jit(solution)/shard_map/collect/pallas_call | solution.py:873
  317.3 0.0 copy-done.1
  317.3 0.0 copy-done.5
  317.3 2.0 fusion.7
  319.3 1.3 broadcast_select_fusion.part
  320.6 11.5 %sum_ends.1 = f32[8,128]{1,0:T(8,128)} custom-call(f32[8,128]{1,0:T(8,128)} %broadcast_select_fusion.part), custom_call_target="tpu_custom_call" | custom-call | tf_op jit(solution)/shard_map/sum_ends/pallas_call | solution.py:921
  332.1 0.7 fusion.21
  332.8 0.7 fusion.20
  333.6 0.7 bitcast_add_fusion
  334.3 0.0 copy-done.2
  334.3 2.3 fusion.3
  (12 shorter events, 0.2 us)
Async XLA Ops:
  0.6 64.3 %copy-start = (bf16[1024,64]{0,1:T(8,128)(2,1)S(1)}, bf16[1024,64]{0,1:T(8,128)(2,1)}, u32[]{:S(2)}) copy-start(bf16[1024,64]{0,1:T(8,128)(2,1)} %param.20) | copy-start | bytes 393220
  2.5 55.6 %copy-start.6 = (s32[128]{0:T(128)}, s32[128]{0:T(128)S(1)}, u32[]{:S(2)}) copy-start(s32[128]{0:T(128)S(1)} %convert_reduce_fusion.firsts) | copy-start | bytes 1540
  4.7 60.3 %copy-start.4 = (f32[1024]{0:T(1024)S(1)}, f32[1024]{0:T(1024)}, u32[]{:S(2)}) copy-start(f32[1024]{0:T(1024)} %param.19) | copy-start | bytes 12292
  235.2 14.2 %copy-start.3 = (f32[72,128]{1,0:T(8,128)S(1)}, f32[72,128]{1,0:T(8,128)}, u32[]{:S(2)}) copy-start(f32[72,128]{1,0:T(8,128)} %get-tuple-element.29) | copy-start | bytes 110596
  250.1 67.1 %copy-start.1 = (bf16[128,1024]{1,0:T(8,128)(2,1)S(1)}, bf16[128,1024]{1,0:T(8,128)(2,1)}, u32[]{:S(2)}) copy-start(bf16[128,1024]{1,0:T(8,128)(2,1)} %attend.1.rows) | copy-start | bytes 786436
  250.1 67.1 %copy-start.5 = (f32[1024]{0:T(1024)S(1)}, f32[1024]{0:T(1024)}, u32[]{:S(2)}) copy-start(f32[1024]{0:T(1024)} %param.19) | copy-start | bytes 12292
  250.1 84.1 %copy-start.2 = (bf16[128,1024]{1,0:T(8,128)(2,1)S(1)}, bf16[128,1024]{1,0:T(8,128)(2,1)}, u32[]{:S(2)}) copy-start(bf16[128,1024]{1,0:T(8,128)(2,1)} %rows.1) | copy-start | bytes 786436
